TPU v7x, 256 devices: a whole 4x4x8 slice. The times are simulated.
256 devices in a mesh: read: 32 (over z_lo, x, core), pos: 8 (over y, z_hi).
Axes of the slice: x: 4, y: 4, z: 8 (z_hi: 2, z_lo: 4; z = z_hi * 4 + z_lo), core: 2. Of those that a mesh axis runs over, the one named last changes fastest.
Arguments:
- features: bfloat16 [128, 256, 768], P('read', 'pos'), may hold values from -6 to 6
- grad_out: bfloat16 [128, 256, 768], P('read', 'pos'), may hold values from -16 to 16
- weights: bfloat16 [4, 768, 768], replicated, may hold values from -0.21875 to 0.21875
- read_start: int32 [128], replicated, may hold values from 0 to 127
- read_end: int32 [128], replicated, may hold values from 129 to 256
Outputs:
- grad_input: bfloat16 [128, 256, 768], P('read', 'pos')
- weight_grads: float32 [768, 3072], P(('read', 'pos'))
Inputs may be any that keep to these rules, and one draw needn't show every extreme that they name: read_end is above read_start for every read.
All inputs are finite; a program needn't handle non-finite values.
Results may differ from a plain program's by a relative error of at most 0.0086.
Values may be sent and summed in bfloat16 or wider, within the bound.
A program may use at most 128 MiB of HBM per device.

v0:
```python
import math

import jax
import jax.numpy as jnp
from jax import lax
from jax.sharding import PartitionSpec as P

HEADS = 12
HEAD_DIM = 64


def coverage(starts, ends, first_col, col_count):
    columns = first_col + jnp.arange(col_count, dtype=jnp.int32)
    inside = (columns[None, :] >= starts[:, None]) & (columns[None, :] < ends[:, None])
    return inside.astype(jnp.float32)


def dot_back(left, right):
    return lax.dot_general(
        left, right, (((1,), (1,)), ((), ())), preferred_element_type=jnp.float32
    )


def project(source, upstream, covered, weights):
    width = source.shape[-1]
    values32 = source.reshape(-1, width).astype(jnp.float32)
    inverse = lax.rsqrt(jnp.mean(values32 * values32, -1, keepdims=True) + 1e-05)
    normed = values32 * inverse
    normed_b = normed.astype(jnp.bfloat16)
    keep_mask = covered.reshape(-1, 1)
    query = (jnp.dot(normed_b, weights[0], preferred_element_type=jnp.float32) * keep_mask).astype(
        jnp.bfloat16
    )
    keys = (jnp.dot(normed_b, weights[1], preferred_element_type=jnp.float32) * keep_mask).astype(
        jnp.bfloat16
    )
    values = (jnp.dot(normed_b, weights[2], preferred_element_type=jnp.float32) * keep_mask).astype(
        jnp.bfloat16
    )
    grad_flat = upstream.reshape(-1, width)
    back_out = dot_back(grad_flat, weights[3]).astype(jnp.bfloat16)
    return (normed, inverse, normed_b, grad_flat, query, keys, values, back_out)


def attend(query, keys, values, back_out, covered, scale):
    reads, narrow, width = query.shape
    shape4 = (reads, narrow, HEADS, HEAD_DIM)
    query4 = query.reshape(shape4)
    keys4 = keys.reshape(shape4)
    values4 = values.reshape(shape4)
    back4 = back_out.reshape(shape4)
    partial_logits = jnp.einsum("rchd,schd->hrs", query4, keys4, preferred_element_type=jnp.float32)
    logits = lax.psum(partial_logits, ("read", "pos")) * scale
    expon = jnp.exp(logits)
    probs = expon / jnp.sum(expon, -1, keepdims=True)
    probs_b = probs.astype(jnp.bfloat16)
    slopes = lax.psum(
        jnp.einsum("rchd,schd->hrs", back4, values4, preferred_element_type=jnp.float32),
        ("read", "pos"),
    )
    mixed = (scale * probs * (slopes - jnp.sum(probs * slopes, -1, keepdims=True))).astype(
        jnp.bfloat16
    )
    output = jnp.einsum(
        "hrs,schd->rchd", probs_b, values4, preferred_element_type=jnp.float32
    ).astype(jnp.bfloat16)
    keep4 = covered[:, :, None, None]
    grad_query = (
        jnp.einsum("hrs,schd->rchd", mixed, keys4, preferred_element_type=jnp.float32) * keep4
    ).astype(jnp.bfloat16)
    grad_keys = (
        jnp.einsum("hrs,rchd->schd", mixed, query4, preferred_element_type=jnp.float32) * keep4
    ).astype(jnp.bfloat16)
    grad_values = (
        jnp.einsum("hrs,rchd->schd", probs_b, back4, preferred_element_type=jnp.float32) * keep4
    ).astype(jnp.bfloat16)
    shape3 = (reads, narrow, width)
    return (
        output.reshape(shape3),
        grad_query.reshape(shape3),
        grad_keys.reshape(shape3),
        grad_values.reshape(shape3),
    )


def input_grad(grad_query, grad_keys, grad_values, weights, normed, inverse):
    grad_norm = (
        dot_back(grad_query, weights[0])
        + dot_back(grad_keys, weights[1])
        + dot_back(grad_values, weights[2])
    )
    result = inverse * (grad_norm - normed * jnp.mean(grad_norm * normed, -1, keepdims=True))
    return result.astype(jnp.bfloat16)


def shards(features, grad_out, weights, read_start, read_end):
    rows, col_dev, width = features.shape
    read_count = lax.axis_size("read")
    pos_count = lax.axis_size("pos")
    read_at = lax.axis_index("read")
    pos_at = lax.axis_index("pos")
    scale = 1.0 / math.sqrt(HEAD_DIM * col_dev * pos_count)
    narrow = col_dev // read_count
    column_first = pos_at * col_dev + read_at * narrow
    column_cover = coverage(read_start, read_end, column_first, narrow)
    starts = lax.dynamic_slice_in_dim(read_start, read_at * rows, rows)
    ends = lax.dynamic_slice_in_dim(read_end, read_at * rows, rows)
    covered = coverage(starts, ends, pos_at * col_dev, col_dev)
    normed, inverse, normed_b, grad_flat, query, keys, values, back_out = project(
        features, grad_out, covered, weights
    )
    token_shape = (rows, col_dev, width)
    col_query, col_keys, col_values, col_back = (
        lax.all_to_all(query.reshape(token_shape), "read", split_axis=1, concat_axis=0, tiled=True),
        lax.all_to_all(keys.reshape(token_shape), "read", split_axis=1, concat_axis=0, tiled=True),
        lax.all_to_all(
            values.reshape(token_shape), "read", split_axis=1, concat_axis=0, tiled=True
        ),
        lax.all_to_all(
            back_out.reshape(token_shape), "read", split_axis=1, concat_axis=0, tiled=True
        ),
    )
    output, grad_query, grad_keys, grad_values = attend(
        col_query, col_keys, col_values, col_back, column_cover, scale
    )
    output, grad_query, grad_keys, grad_values = (
        lax.all_to_all(output, "read", split_axis=0, concat_axis=1, tiled=True),
        lax.all_to_all(grad_query, "read", split_axis=0, concat_axis=1, tiled=True),
        lax.all_to_all(grad_keys, "read", split_axis=0, concat_axis=1, tiled=True),
        lax.all_to_all(grad_values, "read", split_axis=0, concat_axis=1, tiled=True),
    )
    output_flat = output.reshape(-1, width)
    query_flat = grad_query.reshape(-1, width)
    keys_flat = grad_keys.reshape(-1, width)
    values_flat = grad_values.reshape(-1, width)
    grad_input = input_grad(query_flat, keys_flat, values_flat, weights, normed, inverse).reshape(
        token_shape
    )
    right_side = jnp.concatenate([query_flat, keys_flat, values_flat], axis=1)
    inner_part = lax.dot_general(
        normed_b, right_side, (((0,), (0,)), ((), ())), preferred_element_type=jnp.float32
    )
    outer_part = lax.dot_general(
        output_flat, grad_flat, (((0,), (0,)), ((), ())), preferred_element_type=jnp.float32
    )
    weight_grads = lax.psum_scatter(
        jnp.concatenate([inner_part, outer_part], axis=1),
        ("read", "pos"),
        scatter_dimension=0,
        tiled=True,
    )
    return (grad_input, weight_grads)


def solution(mesh):
    in_specs = (P("read", "pos", None), P("read", "pos", None), P(), P(), P())
    out_specs = (P("read", "pos", None), P(("read", "pos"), None))
    return jax.shard_map(shards, mesh=mesh, in_specs=in_specs, out_specs=out_specs, check_vma=False)
```

profile of v0, /device:TPU:1, one launch (start us, length us, event | category | flops | bytes accessed | tf_op | source)
XLA Modules:
  0.0 703.1 jit_solution(4038250459228061290)
XLA Ops:
  7.2 1.1 multiply_reduce_fusion.2
  8.3 1.0 multiply_convert_fusion.2
  11.0 1.6 fusion.16
  12.6 0.8 copy.33
  13.4 10.0 %all-to-all-start = ((bf16[4,32,768]{2,0,1:T(4,128)(2,1)}), bf16[4,32,768]{2,0,1:T(4,128)(2,1)S(1)}, u32[]{:S(2)}, u32[]{:S(2)}) async-start(bf16[4,32,768]{2,0,1:T(4,128)(2,1)} %copy.33), calls=%async_computation | async-start | bytes 393216 | tf_op jit(solution)/shard_map/all_to_all | solution.py:115
  23.4 1.8 fusion.13
  25.2 0.8 copy.37
  26.1 7.0 all-to-all-done
  33.0 3.9 all-to-all-start.2
  36.9 1.6 fusion.22
  38.5 0.8 copy.38
  39.4 7.2 %all-to-all-done.2 = bf16[4,32,768]{2,0,1:T(4,128)(2,1)S(1)} async-done(((bf16[4,32,768]{2,0,1:T(4,128)(2,1)}), bf16[4,32,768]{2,0,1:T(4,128)(2,1)S(1)}, u32[]{:S(2)}, u32[]{:S(2)}) %all-to-all-start.2) | async-done | bytes 196640 | tf_op jit(solution)/shard_map/all_to_all | solution.py:119
  46.5 3.9 all-to-all-start.3
  50.5 1.6 fusion.19
  52.1 0.8 copy.34
  52.9 7.2 %all-to-all-done.3 = bf16[4,32,768]{2,0,1:T(4,128)(2,1)S(1)} async-done(((bf16[4,32,768]{2,0,1:T(4,128)(2,1)}), bf16[4,32,768]{2,0,1:T(4,128)(2,1)S(1)}, u32[]{:S(2)}, u32[]{:S(2)}) %all-to-all-start.3) | async-done | bytes 196640 | tf_op jit(solution)/shard_map/all_to_all | solution.py:116
  60.1 3.9 all-to-all-start.1
  66.2 7.4 %all-to-all-done.1 = bf16[4,32,768]{2,0,1:T(4,128)(2,1)S(1)} async-done(((bf16[4,32,768]{2,0,1:T(4,128)(2,1)}), bf16[4,32,768]{2,0,1:T(4,128)(2,1)S(1)}, u32[]{:S(2)}, u32[]{:S(2)}) %all-to-all-start.1) | async-done | bytes 196640 | tf_op jit(solution)/shard_map/all_to_all | solution.py:114
  74.3 1.2 fusion.49
  75.5 1.2 fusion.48
  76.8 258.8 %all-reduce.7.cloned.1.call-done = (f32[12,128,128]{2,1,0:T(8,128)}, f32[12,128,128]{2,1,0:T(8,128)}) async-done(((f32[12,128,128]{2,1,0:T(8,128)}, f32[12,128,128]{2,1,0:T(8,128)}), (f32[12,128,128]{2,1,0:T(8,128)}, f32[12,128,128]{2,1,0:T(8,128)})) %all-reduce.7.cloned.1.call-update) | async-done | bytes 1572880 | tf_op jit(solution)/shard_map/psum | solution.py:57
  335.6 1.5 fusion.35
  337.1 1.9 multiply_reduce_fusion
  339.0 1.8 multiply_convert_fusion
  342.7 0.8 reshape.206
  343.5 10.0 %all-to-all-start.4 = ((bf16[32,2,1536]{2,1,0:T(2,128)(2,1)}), bf16[32,2,1536]{2,1,0:T(2,128)(2,1)S(1)}, u32[]{:S(2)}, u32[]{:S(2)}) async-start(bf16[32,2,1536]{2,1,0:T(2,128)(2,1)} %reshape.206), calls=%async_computation.4 | async-start | bytes 393216 | tf_op jit(solution)/shard_map/all_to_all | solution.py:128
  354.6 0.8 reshape.208
  355.4 7.7 %all-to-all-done.4 = bf16[32,2,1536]{2,1,0:T(2,128)(2,1)S(1)} async-done(((bf16[32,2,1536]{2,1,0:T(2,128)(2,1)}), bf16[32,2,1536]{2,1,0:T(2,128)(2,1)S(1)}, u32[]{:S(2)}, u32[]{:S(2)}) %all-to-all-start.4) | async-done | bytes 196640 | tf_op jit(solution)/shard_map/all_to_all | solution.py:128
  363.0 3.9 all-to-all-start.5
  368.3 0.8 reshape.210
  369.1 7.4 %all-to-all-done.5 = bf16[32,2,1536]{2,1,0:T(2,128)(2,1)S(1)} async-done(((bf16[32,2,1536]{2,1,0:T(2,128)(2,1)}), bf16[32,2,1536]{2,1,0:T(2,128)(2,1)S(1)}, u32[]{:S(2)}, u32[]{:S(2)}) %all-to-all-start.5) | async-done | bytes 196640 | tf_op jit(solution)/shard_map/all_to_all | solution.py:129
  376.6 3.9 all-to-all-start.6
  382.7 7.4 %all-to-all-done.6 = bf16[32,2,1536]{2,1,0:T(2,128)(2,1)S(1)} async-done(((bf16[32,2,1536]{2,1,0:T(2,128)(2,1)}), bf16[32,2,1536]{2,1,0:T(2,128)(2,1)S(1)}, u32[]{:S(2)}, u32[]{:S(2)}) %all-to-all-start.6) | async-done | bytes 196640 | tf_op jit(solution)/shard_map/all_to_all | solution.py:130
  390.1 3.9 all-to-all-start.7
  394.3 1.2 reduce.1
  395.7 1.2 reduce.2
  397.1 1.2 reduce.3
  398.4 2.5 fusion.7
  400.9 2.7 all-to-all-done.7
  403.8 1.2 reduce.4
  405.5 1.9 convolution_add_fusion.1
  407.4 2.6 fusion.42
  410.0 3.9 fusion.36
  414.0 8.1 %pad_maximum_fusion = f32[768,3072]{1,0:T(8,128)} fusion(f32[768,768]{1,0:T(8,128)S(1)} %fusion.50, f32[768,2304]{1,0:T(8,128)} %fusion.36), kind=kLoop, calls=%fused_computation | loop fusion | flops 2359296 | bytes 18874368 | tf_op jit(solution)/shard_map/concatenate | solution.py:147
  422.1 1.0 copy-done.3
  423.0 0.9 multiply_convert_fusion.1
  423.9 270.8 %all-reduce.5.cloned.1.call-done = f32[768,3072]{1,0:T(8,128)} async-done(((f32[768,3072]{1,0:T(8,128)}), f32[768,3072]{1,0:T(8,128)}) %all-reduce.5.cloned.1.call-update) | async-done | bytes 9437200
  694.7 1.6 constant_dynamic-slice_fusion
  (59 shorter events, 12.4 us)
Async XLA Ops:
  7.2 16.2 %copy-start = (bf16[4,32,768]{2,1,0:T(8,128)(2,1)S(1)}, bf16[4,32,768]{2,1,0:T(8,128)(2,1)}, u32[]{:S(2)}) copy-start(bf16[4,32,768]{2,1,0:T(8,128)(2,1)} %param.6) | copy-start | bytes 589828
  13.4 19.6 %all-to-all-start = ((bf16[4,32,768]{2,0,1:T(4,128)(2,1)}), bf16[4,32,768]{2,0,1:T(4,128)(2,1)S(1)}, u32[]{:S(2)}, u32[]{:S(2)}) async-start(bf16[4,32,768]{2,0,1:T(4,128)(2,1)} %copy.33), calls=%async_computation | async-start | bytes 393216 | tf_op jit(solution)/shard_map/all_to_all | solution.py:115
  33.0 13.5 %all-to-all-start.2 = ((bf16[4,32,768]{2,0,1:T(4,128)(2,1)}), bf16[4,32,768]{2,0,1:T(4,128)(2,1)S(1)}, u32[]{:S(2)}, u32[]{:S(2)}) async-start(bf16[4,32,768]{2,0,1:T(4,128)(2,1)} %copy.37), calls=%async_computation.2 | async-start | bytes 393216 | tf_op jit(solution)/shard_map/all_to_all | solution.py:119
  46.5 13.5 %all-to-all-start.3 = ((bf16[4,32,768]{2,0,1:T(4,128)(2,1)}), bf16[4,32,768]{2,0,1:T(4,128)(2,1)S(1)}, u32[]{:S(2)}, u32[]{:S(2)}) async-start(bf16[4,32,768]{2,0,1:T(4,128)(2,1)} %copy.38), calls=%async_computation.3 | async-start | bytes 393216 | tf_op jit(solution)/shard_map/all_to_all | solution.py:116
  60.1 13.5 %all-to-all-start.1 = ((bf16[4,32,768]{2,0,1:T(4,128)(2,1)}), bf16[4,32,768]{2,0,1:T(4,128)(2,1)S(1)}, u32[]{:S(2)}, u32[]{:S(2)}) async-start(bf16[4,32,768]{2,0,1:T(4,128)(2,1)} %copy.34), calls=%async_computation.1 | async-start | bytes 393216 | tf_op jit(solution)/shard_map/all_to_all | solution.py:114
  64.0 271.6 %all-reduce.7.cloned.1.call-start = ((), (), s32[]{:S(2)}) async-start(), calls=%async_computation.9 | async-start | bytes 3145728 | tf_op jit(solution)/shard_map/psum | solution.py:57
  64.1 12.7 %copy-start.4 = (s32[128]{0:T(128)S(1)}, s32[128]{0:T(128)}, u32[]{:S(2)}) copy-start(s32[128]{0:T(128)} %param.9) | copy-start | bytes 1540
  64.1 12.7 %copy-start.5 = (s32[128]{0:T(128)S(1)}, s32[128]{0:T(128)}, u32[]{:S(2)}) copy-start(s32[128]{0:T(128)} %param.8) | copy-start | bytes 1540
  335.6 31.3 %copy-start.1 = (f32[12,128,128]{2,1,0:T(8,128)S(1)}, f32[12,128,128]{2,1,0:T(8,128)}, u32[]{:S(2)}) copy-start(f32[12,128,128]{2,1,0:T(8,128)} %get-tuple-element.3) | copy-start | bytes 2359300
  343.5 19.6 %all-to-all-start.4 = ((bf16[32,2,1536]{2,1,0:T(2,128)(2,1)}), bf16[32,2,1536]{2,1,0:T(2,128)(2,1)S(1)}, u32[]{:S(2)}, u32[]{:S(2)}) async-start(bf16[32,2,1536]{2,1,0:T(2,128)(2,1)} %reshape.206), calls=%async_computation.4 | async-start | bytes 393216 | tf_op jit(solution)/shard_map/all_to_all | solution.py:128
  363.0 13.5 %all-to-all-start.5 = ((bf16[32,2,1536]{2,1,0:T(2,128)(2,1)}), bf16[32,2,1536]{2,1,0:T(2,128)(2,1)S(1)}, u32[]{:S(2)}, u32[]{:S(2)}) async-start(bf16[32,2,1536]{2,1,0:T(2,128)(2,1)} %reshape.208), calls=%async_computation.5 | async-start | bytes 393216 | tf_op jit(solution)/shard_map/all_to_all | solution.py:129
  376.6 13.5 %all-to-all-start.6 = ((bf16[32,2,1536]{2,1,0:T(2,128)(2,1)}), bf16[32,2,1536]{2,1,0:T(2,128)(2,1)S(1)}, u32[]{:S(2)}, u32[]{:S(2)}) async-start(bf16[32,2,1536]{2,1,0:T(2,128)(2,1)} %reshape.210), calls=%async_computation.6 | async-start | bytes 393216 | tf_op jit(solution)/shard_map/all_to_all | solution.py:130
  390.1 13.5 %all-to-all-start.7 = ((bf16[32,2,1536]{2,1,0:T(2,128)(2,1)}), bf16[32,2,1536]{2,1,0:T(2,128)(2,1)S(1)}, u32[]{:S(2)}, u32[]{:S(2)}) async-start(bf16[32,2,1536]{2,1,0:T(2,128)(2,1)} %reshape.212), calls=%async_computation.7 | async-start | bytes 393216 | tf_op jit(solution)/shard_map/all_to_all | solution.py:127
  394.0 300.7 %all-reduce.5.cloned.1.call-start = ((), (), s32[]{:S(2)}) async-start(), calls=%async_computation.8 | async-start | bytes 18874368
  398.3 9.1 %copy-start.2 = (bf16[4,32,768]{2,1,0:T(8,128)(2,1)S(1)}, bf16[4,32,768]{2,1,0:T(8,128)(2,1)}, u32[]{:S(2)}) copy-start(bf16[4,32,768]{2,1,0:T(8,128)(2,1)} %param.5) | copy-start | bytes 589828
  422.0 1.0 copy-start.3
Sparse Core Ops, SparseCore 0:
  76.9 258.6 all-reduce.6
  422.2 272.4 all-reduce.4
where the time goes:
time: 705 us; the launch traced here: 703 us
  waiting for transfers between devices  584 us (83%)
  starting transfers between devices  43.6 us (6%)
  other arithmetic  24 us (3%)
  matrix products  22 us (3%)
  local copies, waits for them, and re-layouts  15.4 us (2%)
  between operations  14.5 us (2%)
    unnamed x3, waiting for transfers between devices  271 us
    psum x1, waiting for transfers between devices, attend(): lax.psum(jnp.einsum('rchd,schd->hrs', back4, values4, preferred_element_t...  259 us
  transfers between devices with their start and end apart: 10, of which 10 were waited for; matrix products, arithmetic and copies ran while one was open for 3% of the time, Pallas kernels for 0%

commit v1 on v0

v1 whole, which is shorter than its diff:
```python
import math

import jax
import jax.numpy as jnp
from jax import lax
from jax.experimental import pallas as pl
from jax.experimental.pallas import tpu as pltpu
from jax.sharding import PartitionSpec as P

F32, BF16, I32 = jnp.float32, jnp.bfloat16, jnp.int32
D = 768
WIN = 256
READS = 128
SCALE = 1.0 / 128.0
EPS = 1e-05
OWNERS = (0, 3, 5)


def nt(a, b):
    return lax.dot_general(a, b, (((1,), (1,)), ((), ())), preferred_element_type=F32)


def nn(a, b):
    return jnp.dot(a, b, preferred_element_type=F32)


def iota(shape, dim):
    return lax.broadcasted_iota(I32, shape, dim)


def hot(cond):
    return jnp.where(cond, 1.0, 0.0).astype(BF16)


def read_of(g, m):
    zl, xp = lax.div(g, 2), lax.rem(g, 2)
    xi, c = lax.div(m, 2), lax.rem(m, 2)
    return zl * 8 + (xi + xp * (3 - 2 * xi)) * 2 + c


def kernel(
    feat, gout, starts, ends, w_hbm, gin_out, wj_out, w3_out,
    wv, ww, w3, a_buf, fg, fp, gp, nb, heads, lbuf, rl, acc, rz, pm, gr, ob, rg,
    nbt, obt, wg, rw, wz, rwz, fd, rj, r3, gi, ogi,
    s_w, sa_s, sa_r, sc_s, sc_r, sx_s, sx_r, sf_s, sf_r, sl_s, sl_r, sz_s, sz_r,
    sq_s, sq_r, sp_s, sp_r, sg_s, sg_r, sd_s, sd_r, se_s, se_r, sj_s, sj_r, s3_s, s3_r, si_s, si_r,
):
    ri, pi = lax.axis_index("read"), lax.axis_index("pos")
    zl, x, c = lax.div(ri, 8), lax.rem(lax.div(ri, 2), 4), lax.rem(ri, 2)
    xp = lax.div(x, 2)
    xi = x + xp * (3 - 2 * x)
    y, zh = lax.div(pi, 2), lax.rem(pi, 2)
    g, m = zl * 2 + xp, xi * 2 + c
    e, ze = y * 2 + xp, zh * 4 + zl
    par = lax.rem(m, 2)
    off = pl.multiple_of(128 * lax.div(3 * m, 2), 128)
    core_m = xi * 2 + (1 - c)
    side_m = (1 - xi) * 2 + c
    far_m = (1 - xi) * 2 + (1 - c)

    def remote(src, dst, ss, rs, dev):
        return pltpu.make_async_remote_copy(
            src_ref=src, dst_ref=dst, send_sem=ss, recv_sem=rs,
            device_id=dev, device_id_type=pl.DeviceIdType.MESH,
        )

    def mate(mm):
        return (read_of(g, mm), pi)

    def over_g(gg):
        return (read_of(gg, m), pi)

    def over_e(ee):
        return (read_of(zl * 2 + lax.rem(ee, 2), m), lax.div(ee, 2) * 2 + zh)

    def over_z(zz):
        return (read_of(lax.rem(zz, 4) * 2 + xp, m), y * 2 + lax.div(zz, 4))

    def ahead(v, d):
        return lax.rem(v + d, 8)

    def behind(v, d):
        return lax.rem(v + 8 - d, 8)

    turned = (read_of(m * 2 + xp, zl), pi)
    sends = []

    win_copies = [
        pltpu.make_async_copy(w_hbm.at[j, :, pl.ds(off, WIN)], ww.at[j], s_w.at[j]) for j in range(3)
    ]
    win_copies.append(pltpu.make_async_copy(w_hbm.at[3, pl.ds(off, WIN), :], w3, s_w.at[3]))
    full_copies = [pltpu.make_async_copy(w_hbm.at[j], wv.at[j], s_w.at[4 + j]) for j in range(3)]
    for copy in win_copies + full_copies:
        copy.start()

    barrier = pltpu.get_barrier_semaphore()

    def greet(dev):
        pl.semaphore_signal(barrier, inc=1, device_id=dev, device_id_type=pl.DeviceIdType.MESH)

    for d in range(1, 8):
        greet(over_g(ahead(g, d)))
        greet(over_e(ahead(e, d)))
        greet(over_z(ahead(ze, d)))
    for mm in (core_m, side_m, far_m):
        greet(mate(mm))

    @pl.when(zl != m)
    def _():
        greet(turned)

    ro, co = iota((128, 128), 0), iota((128, 128), 1)
    to_groups = hot(co == ((ro >> 2) & 3) * 32 + (ro >> 4) * 4 + (ro & 3))
    for t, ref in ((0, feat), (1, gout)):
        a_buf[t] = nn(to_groups, ref[...].reshape(128, D)).astype(BF16).reshape(8, 16, D)

    @pl.when(zl == m)
    def _():
        pl.semaphore_wait(barrier, 24)

    @pl.when(zl != m)
    def _():
        pl.semaphore_wait(barrier, 25)

    for t in range(2):
        for d in range(1, 8):
            gg = ahead(g, d)
            copy = remote(a_buf.at[t, gg], fg.at[t, m, g], sa_s.at[t, d], sa_r.at[t, d], over_g(gg))
            copy.start()
            sends.append(copy)
        fg[t, m, g] = a_buf[t, g]

    def first(t, d):
        gs = behind(g, d)
        slot = fg.at[t, m, gs]
        if d > 0:
            remote(slot, slot, sa_s.at[t, d], sa_r.at[t, d], over_g(gs)).wait_recv()
        for ss, rs, mm in ((sx_s, sx_r, side_m), (sc_s, sc_r, core_m)):
            copy = remote(slot, slot, ss.at[t, d], rs.at[t, d], mate(mm))
            copy.start()
            sends.append(copy)

    def second(t, d):
        slot = fg.at[t, side_m, behind(g, d)]
        remote(slot, slot, sx_s.at[t, d], sx_r.at[t, d], mate(side_m)).wait_recv()
        copy = remote(slot, slot, sf_s.at[t, d], sf_r.at[t, d], mate(core_m))
        copy.start()
        sends.append(copy)

    def third(t, d):
        slot = fg.at[t, core_m, behind(g, d)]
        remote(slot, slot, sc_s.at[t, d], sc_r.at[t, d], mate(core_m)).wait_recv()
        slot = fg.at[t, far_m, behind(g, d)]
        remote(slot, slot, sf_s.at[t, d], sf_r.at[t, d], mate(core_m)).wait_recv()

    nat = iota((READS, READS), 0)
    gs_v, ms_v, r_v = (nat >> 2) & 7, nat >> 5, nat & 3
    xi_v, xp_v = ms_v >> 1, gs_v & 1
    nat = 4 * ((gs_v >> 1) * 8 + (xi_v + xp_v * (3 - 2 * xi_v)) * 2 + (ms_v & 1)) + r_v
    pick = iota((READS, READS), 1) == nat
    begin = jnp.sum(jnp.where(pick, starts[...].astype(F32), 0.0), axis=1, keepdims=True)
    close = jnp.sum(jnp.where(pick, ends[...].astype(F32), 0.0), axis=1, keepdims=True)

    def cover(k):
        col = (32 * pi + 4 * g + k).astype(F32)
        return jnp.where(col >= begin, 1.0, 0.0) * jnp.where(col < close, 1.0, 0.0)

    def to_columns(k):
        return hot(iota((READS, 512), 1) == iota((READS, 512), 0) * 4 + k)

    for d in range(8):
        first(0, d)
        if d > 0:
            second(0, d - 1)
    second(0, 7)
    for d in range(8):
        third(0, d)
    for copy in win_copies:
        copy.wait()

    for k in range(4):
        f32 = nn(to_columns(k), fg[0].reshape(512, D))
        fp[k] = f32.astype(BF16)
        inverse = lax.rsqrt(jnp.mean(f32 * f32, -1, keepdims=True) + EPS)
        normed_b = (f32 * inverse).astype(BF16)
        nb[k] = normed_b
        keep = cover(k)
        for j in range(3):
            part = (nn(normed_b, ww[j]) * keep).astype(BF16)
            heads[j, 0, :, k * 128 : (k + 1) * 128] = part[:, :128]
            heads[j, 1, :, k * 128 : (k + 1) * 128] = part[:, 128:]
        first(1, 2 * k)
        if k > 0:
            second(1, 2 * k - 1)
        first(1, 2 * k + 1)
        second(1, 2 * k)

    low = jnp.where((iota((1, 512), 1) & 127) < 64, 1.0, 0.0)
    high = 1.0 - low
    par_f = par.astype(F32)
    own = low * (1.0 - par_f) + high * par_f
    plan = ((0, high), (1, low), (par, own))

    def scores(which, left, right):
        for h, (t, mask) in enumerate(plan):
            lbuf[which, h * 128 : (h + 1) * 128, :] = nt(heads[left, t] * mask.astype(BF16), heads[right, t])
        for d in range(1, 8):
            ee = ahead(e, d)
            copy = remote(
                lbuf.at[which, pl.ds(pl.multiple_of(48 * ee, 16), 48), :], rl.at[which, d],
                sl_s.at[which, d], sl_r.at[which, d], over_e(ee),
            )
            copy.start()
            sends.append(copy)

    scores(0, 0, 1)
    second(1, 7)
    for d in range(8):
        third(1, d)
    for k in range(4):
        col_grad = nn(to_columns(k), fg[1].reshape(512, D)).astype(BF16)
        gp[k] = col_grad
        part = nt(col_grad, w3[...]).astype(BF16)
        heads[3, 0, :, k * 128 : (k + 1) * 128] = part[:, :128]
        heads[3, 1, :, k * 128 : (k + 1) * 128] = part[:, 128:]
    scores(1, 3, 2)

    def turn(i, carry):
        w, col = iota((96, D), 0), iota((96, D), 1)
        yy, xx = lax.div(i, 2), lax.rem(i, 2)
        xi2 = (w >> 1) & 1
        row = (
            ((w >> 3) & 3) * 192 + (xi2 + xx * (3 - 2 * xi2)) * 48 + (w & 1) * 24
            + yy * 6 + ((w >> 2) & 1) * 3 + (w >> 5)
        )
        nbt[pl.ds(pl.multiple_of(i * 96, 16), 96), :] = nt(hot(col == row), nb[...].reshape(512, D)).astype(BF16)
        return carry

    lax.fori_loop(0, 8, turn, 0)

    for which in range(2):
        total = lbuf[which, pl.ds(pl.multiple_of(48 * e, 16), 48), :]
        for d in range(1, 8):
            remote(
                rl.at[which, d], rl.at[which, d], sl_s.at[which, d], sl_r.at[which, d], over_e(behind(e, d))
            ).wait_recv()
            total = total + rl[which, d]
        acc[:, which * 128 : (which + 1) * 128] = total

    late = []
    for o, place in enumerate(OWNERS):
        dev = over_z(place)
        copy = remote(acc.at[pl.ds(16 * o, 16), :], rz.at[ze], sz_s.at[o], sz_r.at[ze], dev)

        @pl.when(ze != place)
        def _():
            copy.start()

        late.append((place, copy))

    for o, place in enumerate(OWNERS):
        rows = pl.ds(pl.multiple_of(48 * e + 16 * o, 16), 16)

        @pl.when(ze == place)
        def _():
            total = acc[16 * o : 16 * o + 16, :]
            for s in range(8):
                if s != place:
                    remote(rz.at[s], rz.at[s], sz_s.at[o], sz_r.at[s], over_z(s)).wait_recv()
                    total = total + rz[s]
            expon = jnp.exp(total[:, :128] * SCALE)
            probs = expon / jnp.sum(expon, -1, keepdims=True)
            slopes = total[:, 128:]
            mixed = SCALE * probs * (slopes - jnp.sum(probs * slopes, -1, keepdims=True))
            pm[rows, 0:128] = probs.astype(BF16)
            pm[rows, 128:256] = mixed.astype(BF16)
            out = []
            for s in range(8):
                if s != place:
                    copy = remote(pm.at[rows, :], pm.at[rows, :], sq_s.at[s], sq_r.at[o], over_z(s))
                    copy.start()
                    out.append(copy)
            for copy in out:
                copy.wait_send()

    for o, place in enumerate(OWNERS):
        rows = pl.ds(pl.multiple_of(48 * e + 16 * o, 16), 16)

        @pl.when(ze != place)
        def _():
            remote(pm.at[rows, :], pm.at[rows, :], sq_s.at[0], sq_r.at[o], over_z(place)).wait_recv()

    def chunk(ee):
        return pm.at[pl.ds(pl.multiple_of(48 * ee, 16), 48), :]

    for d in range(1, 8):
        copy = remote(chunk(e), chunk(e), sp_s.at[d], sp_r.at[d], over_e(ahead(e, d)))
        copy.start()
        sends.append(copy)
    keeps = jnp.concatenate([jnp.broadcast_to(cover(k), (READS, 128)) for k in range(4)], axis=1)
    for d in range(1, 8):
        ee = behind(e, d)
        remote(chunk(ee), chunk(ee), sp_s.at[d], sp_r.at[d], over_e(ee)).wait_recv()

    eye = hot(ro == co)
    made = []
    for h, (t, _) in enumerate(plan):
        probs_b = pm[h * 128 : (h + 1) * 128, 0:128]
        mixed = pm[h * 128 : (h + 1) * 128, 128:256]
        made.append(
            (
                nn(mixed, heads[1, t]),
                nn(nt(eye, mixed).astype(BF16), heads[0, t]),
                nn(nt(eye, probs_b).astype(BF16), heads[3, t]),
                nn(probs_b, heads[2, t]),
            )
        )
    for j in range(4):
        tile0 = made[0][j] * high + made[2][j] * (low * (1.0 - par_f))
        tile1 = made[1][j] * low + made[2][j] * (high * par_f)
        for t, tile in ((0, tile0), (1, tile1)):
            if j < 3:
                tile = tile * keeps
            tile = tile.astype(BF16)
            for k in range(4):
                if j < 3:
                    gr[j, k, :, t * 128 : (t + 1) * 128] = tile[:, k * 128 : (k + 1) * 128]
                else:
                    ob[k, :, t * 128 : (t + 1) * 128] = tile[:, k * 128 : (k + 1) * 128]

    def rows_of(mm):
        return pl.ds(pl.multiple_of(32 * mm, 32), 32)

    for d, mm in ((1, side_m), (2, far_m), (3, core_m)):
        copy = remote(gr.at[:, :, rows_of(mm), :], rg.at[m], sg_s.at[d], sg_r.at[d], mate(mm))
        copy.start()
        sends.append(copy)
    rg[m] = gr[:, :, rows_of(m), :]

    ow, cw = iota((256, 256), 0), iota((256, 256), 1)
    u, yy, xx = ow & 31, ow >> 6, (ow >> 5) & 1
    xi2 = (u >> 1) & 1
    local = (
        64 * par + (xi2 + xx * (3 - 2 * xi2)) * 48 + (u & 1) * 24 + yy * 6 + ((u >> 2) & 1) * 3 + (u >> 3)
    )
    obt[...] = nt(hot(jnp.where(u < 24, local, -1) == cw), ob[...].reshape(512, WIN)).astype(BF16)

    def wgrad_copy(d):
        ee = ahead(e, d)
        return remote(wg.at[ee], rw.at[d], sd_s.at[d], sd_r.at[d], over_e(ee))

    def wgrad(d, carry):
        ee = ahead(e, d)
        left = nbt[pl.ds(pl.multiple_of(ee * 96, 16), 96), :]
        for j in range(3):
            wg[ee, 0:96, j * WIN : (j + 1) * WIN] = nn(left, gr[j].reshape(512, WIN)).astype(BF16)
        last = obt[pl.ds(pl.multiple_of(ee * 32, 32), 32), :]
        wg[ee, 96:128, :] = nn(last, gp[...].reshape(512, D)).astype(BF16)

        @pl.when(d < 8)
        def _():
            wgrad_copy(d).start()

        return carry

    lax.fori_loop(1, 9, wgrad, 0)

    for d, mm in ((1, side_m), (2, far_m), (3, core_m)):
        remote(gr.at[:, :, rows_of(mm), :], rg.at[mm], sg_s.at[d], sg_r.at[d], mate(mm)).wait_recv()
    for copy in full_copies:
        copy.wait()
    grad_norm = jnp.zeros((128, D), F32)
    for mm in range(4):
        lane = 128 * ((3 * mm) // 2)
        for j in range(3):
            grad_norm = grad_norm + nt(rg[mm, j].reshape(128, WIN), wv[j, :, lane : lane + WIN])
    mine = fp[:, rows_of(m), :].reshape(128, D).astype(F32)
    inverse = lax.rsqrt(jnp.mean(mine * mine, -1, keepdims=True) + EPS)
    normed = mine * inverse
    result = (inverse * (grad_norm - normed * jnp.mean(grad_norm * normed, -1, keepdims=True))).astype(BF16)
    to_sources = hot(co == (ro & 3) * 32 + (ro >> 2))
    gi[...] = nn(to_sources, result).astype(BF16).reshape(8, 16, D)
    for d in range(1, 8):
        gg = ahead(g, d)
        copy = remote(gi.at[gg], ogi.at[g], si_s.at[d], si_r.at[d], over_g(gg))
        copy.start()
        sends.append(copy)
    ogi[g] = gi[g]

    total = wg[e].astype(F32)
    for d in range(1, 8):
        remote(rw.at[d], rw.at[d], sd_s.at[d], sd_r.at[d], over_e(behind(e, d))).wait_recv()
        total = total + rw[d].astype(F32)
    v, zz = ro & 15, ro >> 4
    src = (v >> 2) * 32 + (zz & 3) * 8 + (zz >> 2) * 4 + (v & 3)
    src = jnp.where(v < 12, src, jnp.where(v < 15, 96 + (v - 12) * 8 + zz, -1))
    wz[...] = nn(hot(co == src), total.astype(BF16)).astype(BF16).reshape(8, 16, D)
    for d in range(1, 8):
        zz2 = ahead(ze, d)
        copy = remote(wz.at[zz2], rwz.at[d], se_s.at[d], se_r.at[d], over_z(zz2))
        copy.start()
        sends.append(copy)

    for d in range(1, 8):
        slot = ogi.at[behind(g, d)]
        remote(slot, slot, si_s.at[d], si_r.at[d], over_g(behind(g, d))).wait_recv()
    from_groups = hot(co == ((ro >> 2) & 7) * 16 + (ro >> 5) * 4 + (ro & 3))
    gin_out[...] = nn(from_groups, ogi[...].reshape(128, D)).astype(BF16).reshape(4, 32, D)

    total = wz[ze].astype(F32)
    for d in range(1, 8):
        remote(rwz.at[d], rwz.at[d], se_s.at[d], se_r.at[d], over_z(behind(ze, d))).wait_recv()
        total = total + rwz[d].astype(F32)
    for mm in range(4):
        for t in range(3):
            fd[mm, t : t + 1, :] = total[t * 4 + mm : t * 4 + mm + 1, :]
        fd[mm, 3:8, :] = jnp.zeros((5, D), F32)
    fd[4, 0:3, :] = total[12:15, :]
    fd[4, 3:8, :] = jnp.zeros((5, D), F32)
    for d, mm in ((1, side_m), (2, far_m), (3, core_m)):
        copy = remote(fd.at[mm], rj.at[m], sj_s.at[d], sj_r.at[d], mate(mm))
        copy.start()
        sends.append(copy)
    rj[m] = fd[m]
    last = remote(fd.at[4], r3, s3_s.at[0], s3_r.at[0], turned)

    @pl.when(zl != m)
    def _():
        last.start()
        last.wait()

    @pl.when(zl == m)
    def _():
        r3[...] = fd[4]

    for d, mm in ((1, side_m), (2, far_m), (3, core_m)):
        remote(fd.at[mm], rj.at[mm], sj_s.at[d], sj_r.at[d], mate(mm)).wait_recv()
    wj_out[...] = rj[...]
    w3_out[...] = r3[...]

    for copy in sends:
        copy.wait_send()
    for d in range(1, 8):
        wgrad_copy(d).wait_send()
    for place, copy in late:

        @pl.when(ze != place)
        def _():
            copy.wait_send()


def shards(features, grad_out, weights, read_start, read_end):
    vm = pl.BlockSpec(memory_space=pltpu.VMEM)
    dma = pltpu.SemaphoreType.DMA
    grad_input, wj, w3 = pl.pallas_call(
        kernel,
        name="tied_rows",
        out_shape=(
            jax.ShapeDtypeStruct((4, 32, D), BF16),
            jax.ShapeDtypeStruct((4, 8, D), F32),
            jax.ShapeDtypeStruct((8, D), F32),
        ),
        in_specs=[vm, vm, vm, vm, pl.BlockSpec(memory_space=pl.ANY)],
        out_specs=(vm, vm, vm),
        scratch_shapes=[
            pltpu.VMEM((3, D, D), BF16),
            pltpu.VMEM((3, D, WIN), BF16),
            pltpu.VMEM((WIN, D), BF16),
            pltpu.VMEM((2, 8, 16, D), BF16),
            pltpu.VMEM((2, 4, 8, 16, D), BF16),
            pltpu.VMEM((4, READS, D), BF16),
            pltpu.VMEM((4, READS, D), BF16),
            pltpu.VMEM((4, READS, D), BF16),
            pltpu.VMEM((4, 2, READS, 512), BF16),
            pltpu.VMEM((2, 384, 128), F32),
            pltpu.VMEM((2, 8, 48, 128), F32),
            pltpu.VMEM((48, 256), F32),
            pltpu.VMEM((8, 16, 256), F32),
            pltpu.VMEM((384, 256), BF16),
            pltpu.VMEM((3, 4, READS, WIN), BF16),
            pltpu.VMEM((4, READS, WIN), BF16),
            pltpu.VMEM((4, 3, 4, 32, WIN), BF16),
            pltpu.VMEM((D, 512), BF16),
            pltpu.VMEM((WIN, 512), BF16),
            pltpu.VMEM((8, 128, D), BF16),
            pltpu.VMEM((8, 128, D), BF16),
            pltpu.VMEM((8, 16, D), BF16),
            pltpu.VMEM((8, 16, D), BF16),
            pltpu.VMEM((5, 8, D), F32),
            pltpu.VMEM((4, 8, D), F32),
            pltpu.VMEM((8, D), F32),
            pltpu.VMEM((8, 16, D), BF16),
            pltpu.VMEM((8, 16, D), BF16),
            dma((7,)),
            dma((2, 8)), dma((2, 8)), dma((2, 8)), dma((2, 8)), dma((2, 8)), dma((2, 8)), dma((2, 8)), dma((2, 8)),
            dma((2, 8)), dma((2, 8)),
            dma((3,)), dma((8,)),
            dma((8,)), dma((3,)),
            dma((8,)), dma((8,)),
            dma((4,)), dma((4,)),
            dma((8,)), dma((8,)),
            dma((8,)), dma((8,)),
            dma((4,)), dma((4,)),
            dma((1,)), dma((1,)),
            dma((8,)), dma((8,)),
        ],
        compiler_params=pltpu.CompilerParams(
            collective_id=0, has_side_effects=True, vmem_limit_bytes=56 * 1024 * 1024
        ),
    )(features, grad_out, read_start.reshape(1, READS), read_end.reshape(1, READS), weights)
    blocks = []
    for j in range(3):
        for mm in range(4):
            at = j * WIN + 64 * (mm % 2)
            blocks.append(wj[mm, 0:3, at : at + 192])
    blocks.append(w3[0:3])
    return (grad_input, jnp.concatenate(blocks, axis=1))


def solution(mesh):
    in_specs = (P("read", "pos", None), P("read", "pos", None), P(), P(), P())
    out_specs = (P("read", "pos", None), P(("read", "pos"), None))
    return jax.shard_map(shards, mesh=mesh, in_specs=in_specs, out_specs=out_specs, check_vma=False)
```

time: 705 us -> 104 us (0.15)
  waiting for transfers between devices: 584 us -> 0 us
  Pallas kernels: 0 us -> 98.9 us
  starting transfers between devices: 43.6 us -> 0 us
  other arithmetic: 24 us -> 0 us
  matrix products: 22 us -> 0 us
  between operations: 14.5 us -> 0.64 us
  local copies, waits for them, and re-layouts: 15.4 us -> 4.01 us
    unnamed x3 -> x0, waiting for transfers between devices: 271 us -> none
    psum x1 -> x0, waiting for transfers between devices: 259 us -> none  [attend(): lax.psum(jnp.einsum('rchd,schd->hrs', back4, values4, preferred_element_t...]
    pallas_call x0 -> x1, Pallas kernels: none -> 98.9 us  [shards(): pl.pallas_call(kernel, name='tied_rows', out_shape=(jax.ShapeDtypeStruct(...]
    all_to_all x8 -> x0, waiting for transfers between devices: 54 us -> none  [the longest x1 7.65 us: shards(): lax.all_to_all(grad_query, 'read', split_axis=0, concat_axis=1, tiled=True)]
    all_to_all x8 -> x0, starting transfers between devices: 43.5 us -> none  [the longest x1 10 us: shards(): lax.all_to_all(keys.reshape(token_shape), 'read', split_axis=1, concat_ax...]
    dot_general x15 -> x0, matrix products: 22 us -> none  [the longest x4 8.82 us: dot_back(): lax.dot_general(left, right, (((1,), (1,)), ((), ())), preferred_element_...]
    concatenate x1 -> x0, other arithmetic: 8.06 us -> none  [shards(): jnp.concatenate([inner_part, outer_part], axis=1)]
  transfers between devices with their start and end apart: 10 -> 0, of which waited for: 10 -> 0; matrix products, arithmetic and copies ran while one was open for 3% -> 0% of each run, Pallas kernels for 0% -> 0%
where the time goes in v1:
time: 104 us
  Pallas kernels  98.9 us (95%)
  local copies, waits for them, and re-layouts  4.01 us (4%)
    pallas_call x1, Pallas kernels, shards(): pl.pallas_call(kernel, name='tied_rows', out_shape=(jax.ShapeDtypeStruct(...  98.9 us

profile of v1, /device:TPU:1, one launch (start us, length us, event | category | flops | bytes accessed | tf_op | source)
XLA Modules:
  0.0 103.5 jit_solution(5948122631697804171)
XLA Ops:
  0.6 98.9 %tied_rows.1 = (bf16[4,32,768]{2,1,0:T(8,128)(2,1)}, f32[4,8,768]{2,1,0:T(8,128)}, f32[8,768]{1,0:T(8,128)}) custom-call(bf16[4,32,768]{2,1,0:T(8,128)(2,1)} %feat.1, bf16[4,32,768]{2,1,0:T(8,128)(2,1)} %gout.1, s32[1,128]{1,0:T(1,128)} %bitcast.26, s32[1,128]{1,0:T(1,128)} %bitcast.27, bf16[4,768,768]{2,1,0:T(8,128)(2,1)} %w_hbm.1), custom_call_target="tpu_custom_call" | custom-call | tf_op jit(solution)/shard_map/tied_rows/pallas_call | solution.py:455
  99.5 0.9 slice_bitcast_fusion
  100.5 0.7 slice.51
  101.2 0.7 concatenate.3
  101.9 1.6 %copy.8 = bf16[4,32,768]{2,1,0:T(8,128)(2,1)} copy(bf16[4,32,768]{2,1,0:T(8,128)(2,1)} %get-tuple-element.22) | data formatting | bytes 393216

commit v2 on v1

--- a/solution.py
+++ b/solution.py
@@ -39,10 +39,10 @@
 
 
 def kernel(
-    feat, gout, starts, ends, w_hbm, gin_out, wj_out, w3_out,
-    wv, ww, w3, a_buf, fg, fp, gp, nb, heads, lbuf, rl, acc, rz, pm, gr, ob, rg,
+    feat_hbm, gout_hbm, starts_hbm, ends_hbm, w_hbm, gin_out, wgrad_out,
+    feat, gout, starts, ends, gin, wsum, wv, ww, w3, a_buf, fg, fp, gp, nb, heads, lbuf, rl, acc, rz, pm, gr, ob, rg,
     nbt, obt, wg, rw, wz, rwz, fd, rj, r3, gi, ogi,
-    s_w, sa_s, sa_r, sc_s, sc_r, sx_s, sx_r, sf_s, sf_r, sl_s, sl_r, sz_s, sz_r,
+    s_in, s_w, sa_s, sa_r, sc_s, sc_r, sx_s, sx_r, sf_s, sf_r, sl_s, sl_r, sz_s, sz_r,
     sq_s, sq_r, sp_s, sp_r, sg_s, sg_r, sd_s, sd_r, se_s, se_r, sj_s, sj_r, s3_s, s3_r, si_s, si_r,
 ):
     ri, pi = lax.axis_index("read"), lax.axis_index("pos")
@@ -85,6 +85,31 @@
     turned = (read_of(m * 2 + xp, zl), pi)
     sends = []
 
+    in_copies = [
+        pltpu.make_async_copy(src, dst, s_in.at[i])
+        for i, (src, dst) in enumerate(
+            ((feat_hbm, feat), (gout_hbm, gout), (starts_hbm, starts), (ends_hbm, ends))
+        )
+    ]
+    for copy in in_copies:
+        copy.start()
+
+    barrier = pltpu.get_barrier_semaphore()
+
+    def greet(dev):
+        pl.semaphore_signal(barrier, inc=1, device_id=dev, device_id_type=pl.DeviceIdType.MESH)
+
+    for d in range(1, 8):
+        greet(over_g(ahead(g, d)))
+        greet(over_e(ahead(e, d)))
+        greet(over_z(ahead(ze, d)))
+    for mm in (core_m, side_m, far_m):
+        greet(mate(mm))
+
+    @pl.when(zl != m)
+    def _():
+        greet(turned)
+
     win_copies = [
         pltpu.make_async_copy(w_hbm.at[j, :, pl.ds(off, WIN)], ww.at[j], s_w.at[j]) for j in range(3)
     ]
@@ -93,21 +118,8 @@
     for copy in win_copies + full_copies:
         copy.start()
 
-    barrier = pltpu.get_barrier_semaphore()
-
-    def greet(dev):
-        pl.semaphore_signal(barrier, inc=1, device_id=dev, device_id_type=pl.DeviceIdType.MESH)
-
-    for d in range(1, 8):
-        greet(over_g(ahead(g, d)))
-        greet(over_e(ahead(e, d)))
-        greet(over_z(ahead(ze, d)))
-    for mm in (core_m, side_m, far_m):
-        greet(mate(mm))
-
-    @pl.when(zl != m)
-    def _():
-        greet(turned)
+    for copy in in_copies:
+        copy.wait()
 
     ro, co = iota((128, 128), 0), iota((128, 128), 1)
     to_groups = hot(co == ((ro >> 2) & 3) * 32 + (ro >> 4) * 4 + (ro & 3))
@@ -130,28 +142,27 @@
             sends.append(copy)
         fg[t, m, g] = a_buf[t, g]
 
-    def first(t, d):
-        gs = behind(g, d)
-        slot = fg.at[t, m, gs]
-        if d > 0:
-            remote(slot, slot, sa_s.at[t, d], sa_r.at[t, d], over_g(gs)).wait_recv()
+    def first(t):
+        for d in range(1, 8):
+            slot = fg.at[t, m, behind(g, d)]
+            remote(slot, slot, sa_s.at[t, d], sa_r.at[t, d], over_g(behind(g, d))).wait_recv()
         for ss, rs, mm in ((sx_s, sx_r, side_m), (sc_s, sc_r, core_m)):
-            copy = remote(slot, slot, ss.at[t, d], rs.at[t, d], mate(mm))
+            copy = remote(fg.at[t, m], fg.at[t, m], ss.at[t], rs.at[t], mate(mm))
             copy.start()
             sends.append(copy)
 
-    def second(t, d):
-        slot = fg.at[t, side_m, behind(g, d)]
-        remote(slot, slot, sx_s.at[t, d], sx_r.at[t, d], mate(side_m)).wait_recv()
-        copy = remote(slot, slot, sf_s.at[t, d], sf_r.at[t, d], mate(core_m))
+    def second(t):
+        slot = fg.at[t, side_m]
+        remote(slot, slot, sx_s.at[t], sx_r.at[t], mate(side_m)).wait_recv()
+        copy = remote(slot, slot, sf_s.at[t], sf_r.at[t], mate(core_m))
         copy.start()
         sends.append(copy)
 
-    def third(t, d):
-        slot = fg.at[t, core_m, behind(g, d)]
-        remote(slot, slot, sc_s.at[t, d], sc_r.at[t, d], mate(core_m)).wait_recv()
-        slot = fg.at[t, far_m, behind(g, d)]
-        remote(slot, slot, sf_s.at[t, d], sf_r.at[t, d], mate(core_m)).wait_recv()
+    def third(t):
+        slot = fg.at[t, core_m]
+        remote(slot, slot, sc_s.at[t], sc_r.at[t], mate(core_m)).wait_recv()
+        slot = fg.at[t, far_m]
+        remote(slot, slot, sf_s.at[t], sf_r.at[t], mate(core_m)).wait_recv()
 
     nat = iota((READS, READS), 0)
     gs_v, ms_v, r_v = (nat >> 2) & 7, nat >> 5, nat & 3
@@ -168,13 +179,10 @@
     def to_columns(k):
         return hot(iota((READS, 512), 1) == iota((READS, 512), 0) * 4 + k)
 
-    for d in range(8):
-        first(0, d)
-        if d > 0:
-            second(0, d - 1)
-    second(0, 7)
-    for d in range(8):
-        third(0, d)
+    first(0)
+    second(0)
+    first(1)
+    third(0)
     for copy in win_copies:
         copy.wait()
 
@@ -189,11 +197,8 @@
             part = (nn(normed_b, ww[j]) * keep).astype(BF16)
             heads[j, 0, :, k * 128 : (k + 1) * 128] = part[:, :128]
             heads[j, 1, :, k * 128 : (k + 1) * 128] = part[:, 128:]
-        first(1, 2 * k)
-        if k > 0:
-            second(1, 2 * k - 1)
-        first(1, 2 * k + 1)
-        second(1, 2 * k)
+        if k == 2:
+            second(1)
 
     low = jnp.where((iota((1, 512), 1) & 127) < 64, 1.0, 0.0)
     high = 1.0 - low
@@ -214,9 +219,7 @@
             sends.append(copy)
 
     scores(0, 0, 1)
-    second(1, 7)
-    for d in range(8):
-        third(1, d)
+    third(1)
     for k in range(4):
         col_grad = nn(to_columns(k), fg[1].reshape(512, D)).astype(BF16)
         gp[k] = col_grad
@@ -405,7 +408,9 @@
         slot = ogi.at[behind(g, d)]
         remote(slot, slot, si_s.at[d], si_r.at[d], over_g(behind(g, d))).wait_recv()
     from_groups = hot(co == ((ro >> 2) & 7) * 16 + (ro >> 5) * 4 + (ro & 3))
-    gin_out[...] = nn(from_groups, ogi[...].reshape(128, D)).astype(BF16).reshape(4, 32, D)
+    gin[...] = nn(from_groups, ogi[...].reshape(128, D)).astype(BF16).reshape(4, 32, D)
+    gin_copy = pltpu.make_async_copy(gin, gin_out, s_in.at[0])
+    gin_copy.start()
 
     total = wz[ze].astype(F32)
     for d in range(1, 8):
@@ -435,11 +440,22 @@
 
     for d, mm in ((1, side_m), (2, far_m), (3, core_m)):
         remote(fd.at[mm], rj.at[mm], sj_s.at[d], sj_r.at[d], mate(mm)).wait_recv()
-    wj_out[...] = rj[...]
-    w3_out[...] = r3[...]
+    for j in range(3):
+        for tile in range(6):
+            value = jnp.zeros((3, 128), F32)
+            for mm in range(4):
+                at = tile - (3 * mm) // 2
+                if at in (0, 1):
+                    value = value + rj[mm, 0:3, j * WIN + at * 128 : j * WIN + (at + 1) * 128]
+            wsum[:, j * D + tile * 128 : j * D + (tile + 1) * 128] = value
+    wsum[:, 3 * D : 4 * D] = r3[0:3, :]
+    wsum_copy = pltpu.make_async_copy(wsum, wgrad_out, s_in.at[1])
+    wsum_copy.start()
 
     for copy in sends:
         copy.wait_send()
+    gin_copy.wait()
+    wsum_copy.wait()
     for d in range(1, 8):
         wgrad_copy(d).wait_send()
     for place, copy in late:
@@ -450,19 +466,24 @@
 
 
 def shards(features, grad_out, weights, read_start, read_end):
-    vm = pl.BlockSpec(memory_space=pltpu.VMEM)
+    hbm = pl.BlockSpec(memory_space=pl.ANY)
     dma = pltpu.SemaphoreType.DMA
-    grad_input, wj, w3 = pl.pallas_call(
+    return pl.pallas_call(
         kernel,
         name="tied_rows",
         out_shape=(
             jax.ShapeDtypeStruct((4, 32, D), BF16),
-            jax.ShapeDtypeStruct((4, 8, D), F32),
-            jax.ShapeDtypeStruct((8, D), F32),
+            jax.ShapeDtypeStruct((3, 4 * D), F32),
         ),
-        in_specs=[vm, vm, vm, vm, pl.BlockSpec(memory_space=pl.ANY)],
-        out_specs=(vm, vm, vm),
+        in_specs=[hbm] * 5,
+        out_specs=(hbm, hbm),
         scratch_shapes=[
+            pltpu.VMEM((4, 32, D), BF16),
+            pltpu.VMEM((4, 32, D), BF16),
+            pltpu.VMEM((1, READS), I32),
+            pltpu.VMEM((1, READS), I32),
+            pltpu.VMEM((4, 32, D), BF16),
+            pltpu.VMEM((3, 4 * D), F32),
             pltpu.VMEM((3, D, D), BF16),
             pltpu.VMEM((3, D, WIN), BF16),
             pltpu.VMEM((WIN, D), BF16),
@@ -491,8 +512,8 @@
             pltpu.VMEM((8, D), F32),
             pltpu.VMEM((8, 16, D), BF16),
             pltpu.VMEM((8, 16, D), BF16),
-            dma((7,)),
-            dma((2, 8)), dma((2, 8)), dma((2, 8)), dma((2, 8)), dma((2, 8)), dma((2, 8)), dma((2, 8)), dma((2, 8)),
+            dma((4,)), dma((7,)),
+            dma((2, 8)), dma((2, 8)), dma((2,)), dma((2,)), dma((2,)), dma((2,)), dma((2,)), dma((2,)),
             dma((2, 8)), dma((2, 8)),
             dma((3,)), dma((8,)),
             dma((8,)), dma((3,)),
@@ -508,13 +529,6 @@
             collective_id=0, has_side_effects=True, vmem_limit_bytes=56 * 1024 * 1024
         ),
     )(features, grad_out, read_start.reshape(1, READS), read_end.reshape(1, READS), weights)
-    blocks = []
-    for j in range(3):
-        for mm in range(4):
-            at = j * WIN + 64 * (mm % 2)
-            blocks.append(wj[mm, 0:3, at : at + 192])
-    blocks.append(w3[0:3])
-    return (grad_input, jnp.concatenate(blocks, axis=1))
 
 
 def solution(mesh):

time: 104 us -> 90.4 us (0.87)
  Pallas kernels: 98.9 us -> 86 us
    pallas_call x1, Pallas kernels: 98.9 us -> 86 us  [shards(): pl.pallas_call(kernel, name='tied_rows', out_shape=(jax.ShapeDtypeStruct(...]
    unnamed x1 -> x2, local copies, waits for them, and re-layouts: 1.62 us -> 3.04 us
where the time goes in v2:
time: 90.4 us; the launch traced here: 89.6 us
  Pallas kernels  86 us (95%)
  local copies, waits for them, and re-layouts  3.04 us (3%)
    pallas_call x1, Pallas kernels, shards(): pl.pallas_call(kernel, name='tied_rows', out_shape=(jax.ShapeDtypeStruct(...  86 us
    unnamed x2, local copies, waits for them, and re-layouts  3.04 us

profile of v2, /device:TPU:1, one launch (start us, length us, event | category | flops | bytes accessed | tf_op | source)
XLA Modules:
  0.0 89.6 jit_solution(4390355627375111430)
XLA Ops:
  0.6 86.0 %tied_rows.1 = (bf16[4,32,768]{2,1,0:T(8,128)(2,1)}, f32[3,3072]{1,0:T(4,128)}) custom-call(bf16[4,32,768]{2,1,0:T(8,128)(2,1)} %feat_hbm.1, bf16[4,32,768]{2,1,0:T(8,128)(2,1)} %gout_hbm.1, s32[1,128]{1,0:T(1,128)} %bitcast.2, s32[1,128]{1,0:T(1,128)} %bitcast.3, bf16[4,768,768]{2,1,0:T(8,128)(2,1)} %w_hbm.1), custom_call_target="tpu_custom_call" | custom-call | tf_op jit(solution)/shard_map/tied_rows/pallas_call | solution.py:471
  86.6 1.6 %copy.9 = bf16[4,32,768]{2,1,0:T(8,128)(2,1)} copy(bf16[4,32,768]{2,1,0:T(8,128)(2,1)} %get-tuple-element.4) | data formatting | bytes 393216
  88.2 1.4 %copy.10 = f32[3,3072]{1,0:T(4,128)} copy(f32[3,3072]{1,0:T(4,128)} %get-tuple-element.5) | data formatting | bytes 73728

commit v3 on v2

--- a/solution.py
+++ b/solution.py
@@ -10,6 +10,7 @@
 F32, BF16, I32 = jnp.float32, jnp.bfloat16, jnp.int32
 D = 768
 WIN = 256
+PACK = 640
 READS = 128
 SCALE = 1.0 / 128.0
 EPS = 1e-05
@@ -40,10 +41,10 @@
 
 def kernel(
     feat_hbm, gout_hbm, starts_hbm, ends_hbm, w_hbm, gin_out, wgrad_out,
-    feat, gout, starts, ends, gin, wsum, wv, ww, w3, a_buf, fg, fp, gp, nb, heads, lbuf, rl, acc, rz, pm, gr, ob, rg,
-    nbt, obt, wg, rw, wz, rwz, fd, rj, r3, gi, ogi,
+    feat, gout, starts, ends, gin, wsum, wv, ww, w3, a_buf, fg, fp, gp, nb, heads, lbuf, rl, acc, rz, pm,
+    gr, gpk, ob, rg, nbt, obt, wa, ra, wb, rb, za, rza, yb, ryb, fd, rj, f3, r3, gi, ogi,
     s_in, s_w, sa_s, sa_r, sc_s, sc_r, sx_s, sx_r, sf_s, sf_r, sl_s, sl_r, sz_s, sz_r,
-    sq_s, sq_r, sp_s, sp_r, sg_s, sg_r, sd_s, sd_r, se_s, se_r, sj_s, sj_r, s3_s, s3_r, si_s, si_r,
+    sq_s, sq_r, sp_s, sp_r, sg_s, sg_r, sd_s, sd_r, se_s, se_r, sb_s, sb_r, sy_s, sy_r, sj_s, sj_r, s3_s, s3_r, si_s, si_r,
 ):
     ri, pi = lax.axis_index("read"), lax.axis_index("pos")
     zl, x, c = lax.div(ri, 8), lax.rem(lax.div(ri, 2), 4), lax.rem(ri, 2)
@@ -220,17 +221,16 @@
 
     scores(0, 0, 1)
     third(1)
+    back = nt(fg[1].reshape(512, D), w3[...]).astype(BF16)
     for k in range(4):
-        col_grad = nn(to_columns(k), fg[1].reshape(512, D)).astype(BF16)
-        gp[k] = col_grad
-        part = nt(col_grad, w3[...]).astype(BF16)
+        part = nn(to_columns(k), back).astype(BF16)
         heads[3, 0, :, k * 128 : (k + 1) * 128] = part[:, :128]
         heads[3, 1, :, k * 128 : (k + 1) * 128] = part[:, 128:]
     scores(1, 3, 2)
 
     def turn(i, carry):
         w, col = iota((96, D), 0), iota((96, D), 1)
-        yy, xx = lax.div(i, 2), lax.rem(i, 2)
+        yy, xx = lax.div(ahead(e, i + 1), 2), lax.rem(ahead(e, i + 1), 2)
         xi2 = (w >> 1) & 1
         row = (
             ((w >> 3) & 3) * 192 + (xi2 + xx * (3 - 2 * xi2)) * 48 + (w & 1) * 24
@@ -240,6 +240,8 @@
         return carry
 
     lax.fori_loop(0, 8, turn, 0)
+    for k in range(4):
+        gp[k] = nn(to_columns(k), fg[1].reshape(512, D)).astype(BF16)
 
     for which in range(2):
         total = lbuf[which, pl.ds(pl.multiple_of(48 * e, 16), 48), :]
@@ -318,18 +320,28 @@
                 nn(probs_b, heads[2, t]),
             )
         )
+    def lanes(v, k):
+        return v[:, k * 128 : (k + 1) * 128]
+
+    spare = []
     for j in range(4):
         tile0 = made[0][j] * high + made[2][j] * (low * (1.0 - par_f))
         tile1 = made[1][j] * low + made[2][j] * (high * par_f)
-        for t, tile in ((0, tile0), (1, tile1)):
+        if j < 3:
+            tile0, tile1 = tile0 * keeps, tile1 * keeps
+            full = (tile0 * (1.0 - par_f) + tile1 * par_f).astype(BF16)
+            spare.append(tile1 * (1.0 - par_f) + tile0 * par_f)
+        for k in range(4):
+            for t, tile in ((0, tile0), (1, tile1)):
+                if j < 3:
+                    gr[j, k, :, t * 128 : (t + 1) * 128] = lanes(tile, k).astype(BF16)
+                else:
+                    ob[k, :, t * 128 : (t + 1) * 128] = lanes(tile, k).astype(BF16)
             if j < 3:
-                tile = tile * keeps
-            tile = tile.astype(BF16)
-            for k in range(4):
-                if j < 3:
-                    gr[j, k, :, t * 128 : (t + 1) * 128] = tile[:, k * 128 : (k + 1) * 128]
-                else:
-                    ob[k, :, t * 128 : (t + 1) * 128] = tile[:, k * 128 : (k + 1) * 128]
+                gpk[k, :, j * 128 : (j + 1) * 128] = lanes(full, k)
+    for k in range(4):
+        gpk[k, :, 384:512] = (lanes(spare[0], k) + pltpu.roll(lanes(spare[1], k), 64, axis=1)).astype(BF16)
+        gpk[k, :, 512:640] = lanes(spare[2], k).astype(BF16)
 
     def rows_of(mm):
         return pl.ds(pl.multiple_of(32 * mm, 32), 32)
@@ -340,33 +352,29 @@
         sends.append(copy)
     rg[m] = gr[:, :, rows_of(m), :]
 
+    right = gpk[...].reshape(512, PACK)
+    for half in range(2):
+        part = nn(nbt[half * 384 : (half + 1) * 384, :], right).astype(BF16)
+        for q in range(4):
+            d = (half * 4 + q + 1) % 8
+            wa[d] = part[q * 96 : (q + 1) * 96, :]
+        for q in range(4):
+            d = (half * 4 + q + 1) % 8
+            if d > 0:
+                copy = remote(wa.at[d], ra.at[d], sd_s.at[d], sd_r.at[d], over_e(ahead(e, d)))
+                copy.start()
+                sends.append(copy)
+
     ow, cw = iota((256, 256), 0), iota((256, 256), 1)
-    u, yy, xx = ow & 31, ow >> 6, (ow >> 5) & 1
-    xi2 = (u >> 1) & 1
-    local = (
-        64 * par + (xi2 + xx * (3 - 2 * xi2)) * 48 + (u & 1) * 24 + yy * 6 + ((u >> 2) & 1) * 3 + (u >> 3)
-    )
+    u, zz = ow & 31, ((ow >> 5) + ze) & 7
+    xi2, xx, yy = (zz >> 1) & 1, u & 1, (u >> 1) & 3
+    local = 64 * par + (xi2 + xx * (3 - 2 * xi2)) * 48 + (zz & 1) * 24 + yy * 6 + (zz >> 2) * 3 + (u >> 3)
     obt[...] = nt(hot(jnp.where(u < 24, local, -1) == cw), ob[...].reshape(512, WIN)).astype(BF16)
-
-    def wgrad_copy(d):
-        ee = ahead(e, d)
-        return remote(wg.at[ee], rw.at[d], sd_s.at[d], sd_r.at[d], over_e(ee))
-
-    def wgrad(d, carry):
-        ee = ahead(e, d)
-        left = nbt[pl.ds(pl.multiple_of(ee * 96, 16), 96), :]
-        for j in range(3):
-            wg[ee, 0:96, j * WIN : (j + 1) * WIN] = nn(left, gr[j].reshape(512, WIN)).astype(BF16)
-        last = obt[pl.ds(pl.multiple_of(ee * 32, 32), 32), :]
-        wg[ee, 96:128, :] = nn(last, gp[...].reshape(512, D)).astype(BF16)
-
-        @pl.when(d < 8)
-        def _():
-            wgrad_copy(d).start()
-
-        return carry
-
-    lax.fori_loop(1, 9, wgrad, 0)
+    wb[...] = nn(obt[...], gp[...].reshape(512, D)).astype(BF16).reshape(8, 32, D)
+    for d in range(1, 8):
+        copy = remote(wb.at[d], rb.at[d], sb_s.at[d], sb_r.at[d], over_z(ahead(ze, d)))
+        copy.start()
+        sends.append(copy)
 
     for d, mm in ((1, side_m), (2, far_m), (3, core_m)):
         remote(gr.at[:, :, rows_of(mm), :], rg.at[mm], sg_s.at[d], sg_r.at[d], mate(mm)).wait_recv()
@@ -390,17 +398,29 @@
         sends.append(copy)
     ogi[g] = gi[g]
 
-    total = wg[e].astype(F32)
-    for d in range(1, 8):
-        remote(rw.at[d], rw.at[d], sd_s.at[d], sd_r.at[d], over_e(behind(e, d))).wait_recv()
-        total = total + rw[d].astype(F32)
-    v, zz = ro & 15, ro >> 4
-    src = (v >> 2) * 32 + (zz & 3) * 8 + (zz >> 2) * 4 + (v & 3)
-    src = jnp.where(v < 12, src, jnp.where(v < 15, 96 + (v - 12) * 8 + zz, -1))
-    wz[...] = nn(hot(co == src), total.astype(BF16)).astype(BF16).reshape(8, 16, D)
-    for d in range(1, 8):
-        zz2 = ahead(ze, d)
-        copy = remote(wz.at[zz2], rwz.at[d], se_s.at[d], se_r.at[d], over_z(zz2))
+    total = wb[0].astype(F32)
+    for d in range(1, 8):
+        remote(rb.at[d], rb.at[d], sb_s.at[d], sb_r.at[d], over_z(behind(ze, d))).wait_recv()
+        total = total + rb[d].astype(F32)
+    rb_row, rb_col = iota((128, 32), 0), iota((128, 32), 1)
+    v = rb_row & 15
+    src = jnp.where(v < 3, v * 8 + (((rb_row >> 4) + e) & 7), -1)
+    yb[...] = nn(hot(rb_col == src), total.astype(BF16)).astype(BF16).reshape(8, 16, D)
+    for d in range(1, 8):
+        copy = remote(yb.at[d], ryb.at[d], sy_s.at[d], sy_r.at[d], over_e(ahead(e, d)))
+        copy.start()
+        sends.append(copy)
+
+    total = wa[0].astype(F32)
+    for d in range(1, 8):
+        remote(ra.at[d], ra.at[d], sd_s.at[d], sd_r.at[d], over_e(behind(e, d))).wait_recv()
+        total = total + ra[d].astype(F32)
+    ra_row, ra_col = iota((128, 96), 0), iota((128, 96), 1)
+    v, zz = ra_row & 15, ((ra_row >> 4) + ze) & 7
+    src = jnp.where(v < 12, (v >> 2) * 32 + (zz & 3) * 8 + (zz >> 2) * 4 + (v & 3), -1)
+    za[...] = nn(hot(ra_col == src), total.astype(BF16)).astype(BF16).reshape(8, 16, PACK)
+    for d in range(1, 8):
+        copy = remote(za.at[d], rza.at[d], se_s.at[d], se_r.at[d], over_z(ahead(ze, d)))
         copy.start()
         sends.append(copy)
 
@@ -412,42 +432,54 @@
     gin_copy = pltpu.make_async_copy(gin, gin_out, s_in.at[0])
     gin_copy.start()
 
-    total = wz[ze].astype(F32)
-    for d in range(1, 8):
-        remote(rwz.at[d], rwz.at[d], se_s.at[d], se_r.at[d], over_z(behind(ze, d))).wait_recv()
-        total = total + rwz[d].astype(F32)
+    total = yb[0].astype(F32)
+    for d in range(1, 8):
+        remote(ryb.at[d], ryb.at[d], sy_s.at[d], sy_r.at[d], over_e(behind(e, d))).wait_recv()
+        total = total + ryb[d].astype(F32)
+    f3[...] = total[0:8, :]
+    last = remote(f3, r3, s3_s.at[0], s3_r.at[0], turned)
+
+    @pl.when(zl != m)
+    def _():
+        last.start()
+
+    @pl.when(zl == m)
+    def _():
+        r3[...] = f3[...]
+
+    total = za[0].astype(F32)
+    for d in range(1, 8):
+        remote(rza.at[d], rza.at[d], se_s.at[d], se_r.at[d], over_z(behind(ze, d))).wait_recv()
+        total = total + rza[d].astype(F32)
     for mm in range(4):
         for t in range(3):
             fd[mm, t : t + 1, :] = total[t * 4 + mm : t * 4 + mm + 1, :]
-        fd[mm, 3:8, :] = jnp.zeros((5, D), F32)
-    fd[4, 0:3, :] = total[12:15, :]
-    fd[4, 3:8, :] = jnp.zeros((5, D), F32)
+        fd[mm, 3:8, :] = jnp.zeros((5, PACK), F32)
     for d, mm in ((1, side_m), (2, far_m), (3, core_m)):
         copy = remote(fd.at[mm], rj.at[m], sj_s.at[d], sj_r.at[d], mate(mm))
         copy.start()
         sends.append(copy)
     rj[m] = fd[m]
-    last = remote(fd.at[4], r3, s3_s.at[0], s3_r.at[0], turned)
 
     @pl.when(zl != m)
     def _():
-        last.start()
         last.wait()
-
-    @pl.when(zl == m)
-    def _():
-        r3[...] = fd[4]
 
     for d, mm in ((1, side_m), (2, far_m), (3, core_m)):
         remote(fd.at[mm], rj.at[mm], sj_s.at[d], sj_r.at[d], mate(mm)).wait_recv()
     for j in range(3):
+        tiles = [jnp.zeros((3, 128), F32)] * 6
+        for mm in range(4):
+            side = (low, high)[mm % 2][:, :128]
+            full = rj[mm, :, j * 128 : (j + 1) * 128]
+            rest = rj[mm, :, (512 if j == 2 else 384) : (640 if j == 2 else 512)]
+            if j == 1:
+                rest = pltpu.roll(rest, 64, axis=1)
+            pair = (full, rest * side) if mm % 2 == 0 else (rest * side, full)
+            for at in range(2):
+                tiles[(3 * mm) // 2 + at] = tiles[(3 * mm) // 2 + at] + pair[at][0:3]
         for tile in range(6):
-            value = jnp.zeros((3, 128), F32)
-            for mm in range(4):
-                at = tile - (3 * mm) // 2
-                if at in (0, 1):
-                    value = value + rj[mm, 0:3, j * WIN + at * 128 : j * WIN + (at + 1) * 128]
-            wsum[:, j * D + tile * 128 : j * D + (tile + 1) * 128] = value
+            wsum[:, j * D + tile * 128 : j * D + (tile + 1) * 128] = tiles[tile]
     wsum[:, 3 * D : 4 * D] = r3[0:3, :]
     wsum_copy = pltpu.make_async_copy(wsum, wgrad_out, s_in.at[1])
     wsum_copy.start()
@@ -456,8 +488,6 @@
         copy.wait_send()
     gin_copy.wait()
     wsum_copy.wait()
-    for d in range(1, 8):
-        wgrad_copy(d).wait_send()
     for place, copy in late:
 
         @pl.when(ze != place)
@@ -499,16 +529,22 @@
             pltpu.VMEM((8, 16, 256), F32),
             pltpu.VMEM((384, 256), BF16),
             pltpu.VMEM((3, 4, READS, WIN), BF16),
+            pltpu.VMEM((4, READS, PACK), BF16),
             pltpu.VMEM((4, READS, WIN), BF16),
             pltpu.VMEM((4, 3, 4, 32, WIN), BF16),
             pltpu.VMEM((D, 512), BF16),
             pltpu.VMEM((WIN, 512), BF16),
-            pltpu.VMEM((8, 128, D), BF16),
-            pltpu.VMEM((8, 128, D), BF16),
+            pltpu.VMEM((8, 96, PACK), BF16),
+            pltpu.VMEM((8, 96, PACK), BF16),
+            pltpu.VMEM((8, 32, D), BF16),
+            pltpu.VMEM((8, 32, D), BF16),
+            pltpu.VMEM((8, 16, PACK), BF16),
+            pltpu.VMEM((8, 16, PACK), BF16),
             pltpu.VMEM((8, 16, D), BF16),
             pltpu.VMEM((8, 16, D), BF16),
-            pltpu.VMEM((5, 8, D), F32),
-            pltpu.VMEM((4, 8, D), F32),
+            pltpu.VMEM((4, 8, PACK), F32),
+            pltpu.VMEM((4, 8, PACK), F32),
+            pltpu.VMEM((8, D), F32),
             pltpu.VMEM((8, D), F32),
             pltpu.VMEM((8, 16, D), BF16),
             pltpu.VMEM((8, 16, D), BF16),
@@ -521,6 +557,8 @@
             dma((4,)), dma((4,)),
             dma((8,)), dma((8,)),
             dma((8,)), dma((8,)),
+            dma((8,)), dma((8,)),
+            dma((8,)), dma((8,)),
             dma((4,)), dma((4,)),
             dma((1,)), dma((1,)),
             dma((8,)), dma((8,)),

time: 90.4 us -> 83.8 us (0.927)
  Pallas kernels: 86 us -> 80 us
    pallas_call x1, Pallas kernels: 86 us -> 80 us  [shards(): pl.pallas_call(kernel, name='tied_rows', out_shape=(jax.ShapeDtypeStruct(...]
where the time goes in v3:
time: 83.8 us; the launch traced here: 83.6 us
  Pallas kernels  80 us (95%)
  local copies, waits for them, and re-layouts  3.04 us (4%)
    pallas_call x1, Pallas kernels, shards(): pl.pallas_call(kernel, name='tied_rows', out_shape=(jax.ShapeDtypeStruct(...  80 us
    unnamed x2, local copies, waits for them, and re-layouts  3.04 us

profile of v3, /device:TPU:1, one launch (start us, length us, event | category | flops | bytes accessed | tf_op | source)
XLA Modules:
  0.0 83.6 jit_solution(2676376478879109235)
XLA Ops:
  0.6 80.0 %tied_rows.1 = (bf16[4,32,768]{2,1,0:T(8,128)(2,1)}, f32[3,3072]{1,0:T(4,128)}) custom-call(bf16[4,32,768]{2,1,0:T(8,128)(2,1)} %feat_hbm.1, bf16[4,32,768]{2,1,0:T(8,128)(2,1)} %gout_hbm.1, s32[1,128]{1,0:T(1,128)} %bitcast.2, s32[1,128]{1,0:T(1,128)} %bitcast.3, bf16[4,768,768]{2,1,0:T(8,128)(2,1)} %w_hbm.1), custom_call_target="tpu_custom_call" | custom-call | tf_op jit(solution)/shard_map/tied_rows/pallas_call | solution.py:501
  80.6 1.6 %copy.9 = bf16[4,32,768]{2,1,0:T(8,128)(2,1)} copy(bf16[4,32,768]{2,1,0:T(8,128)(2,1)} %get-tuple-element.4) | data formatting | bytes 393216
  82.2 1.4 %copy.10 = f32[3,3072]{1,0:T(4,128)} copy(f32[3,3072]{1,0:T(4,128)} %get-tuple-element.5) | data formatting | bytes 73728

commit v4 on v3

--- a/solution.py
+++ b/solution.py
@@ -40,10 +40,10 @@
 
 
 def kernel(
-    feat_hbm, gout_hbm, starts_hbm, ends_hbm, w_hbm, gin_out, wgrad_out,
-    feat, gout, starts, ends, gin, wsum, wv, ww, w3, a_buf, fg, fp, gp, nb, heads, lbuf, rl, acc, rz, pm,
+    feat_hbm, gout_hbm, starts_hbm, ends_hbm, w_hbm, gin, wsum,
+    feat, gout, starts, ends, wv, ww, w3, a_buf, fg, bg, bx, qa, na, mine, gp, nb, heads, lbuf, rl, acc, rz, pm,
     gr, gpk, ob, rg, nbt, obt, wa, ra, wb, rb, za, rza, yb, ryb, fd, rj, f3, r3, gi, ogi,
-    s_in, s_w, sa_s, sa_r, sc_s, sc_r, sx_s, sx_r, sf_s, sf_r, sl_s, sl_r, sz_s, sz_r,
+    s_in, s_w, sa_s, sa_r, sh_s, sh_r, sc_s, sc_r, sx_s, sx_r, sf_s, sf_r, sl_s, sl_r, sz_s, sz_r,
     sq_s, sq_r, sp_s, sp_r, sg_s, sg_r, sd_s, sd_r, se_s, se_r, sb_s, sb_r, sy_s, sy_r, sj_s, sj_r, s3_s, s3_r, si_s, si_r,
 ):
     ri, pi = lax.axis_index("read"), lax.axis_index("pos")
@@ -114,18 +114,31 @@
     win_copies = [
         pltpu.make_async_copy(w_hbm.at[j, :, pl.ds(off, WIN)], ww.at[j], s_w.at[j]) for j in range(3)
     ]
-    win_copies.append(pltpu.make_async_copy(w_hbm.at[3, pl.ds(off, WIN), :], w3, s_w.at[3]))
+    w3_copy = pltpu.make_async_copy(w_hbm.at[3], w3, s_w.at[3])
     full_copies = [pltpu.make_async_copy(w_hbm.at[j], wv.at[j], s_w.at[4 + j]) for j in range(3)]
-    for copy in win_copies + full_copies:
-        copy.start()
-
-    for copy in in_copies:
-        copy.wait()
+    for copy in [w3_copy] + win_copies + full_copies:
+        copy.start()
 
     ro, co = iota((128, 128), 0), iota((128, 128), 1)
     to_groups = hot(co == ((ro >> 2) & 3) * 32 + (ro >> 4) * 4 + (ro & 3))
-    for t, ref in ((0, feat), (1, gout)):
-        a_buf[t] = nn(to_groups, ref[...].reshape(128, D)).astype(BF16).reshape(8, 16, D)
+    def by_group(ref):
+        return nn(to_groups, ref[...].reshape(128, D)).astype(BF16)
+
+    def spread(i, dst):
+        for d in range(1, 8):
+            gg = ahead(g, d)
+            copy = remote(a_buf.at[i, gg], dst.at[g], sa_s.at[i, d], sa_r.at[i, d], over_g(gg))
+            copy.start()
+            sends.append(copy)
+        dst[g] = a_buf[i, g]
+
+    def gathered(i, dst):
+        for d in range(1, 8):
+            slot = dst.at[behind(g, d)]
+            remote(slot, slot, sa_s.at[i, d], sa_r.at[i, d], over_g(behind(g, d))).wait_recv()
+
+    in_copies[0].wait()
+    a_buf[0] = by_group(feat).reshape(8, 16, D)
 
     @pl.when(zl == m)
     def _():
@@ -135,18 +148,17 @@
     def _():
         pl.semaphore_wait(barrier, 25)
 
-    for t in range(2):
-        for d in range(1, 8):
-            gg = ahead(g, d)
-            copy = remote(a_buf.at[t, gg], fg.at[t, m, g], sa_s.at[t, d], sa_r.at[t, d], over_g(gg))
-            copy.start()
-            sends.append(copy)
-        fg[t, m, g] = a_buf[t, g]
+    spread(0, fg.at[0, m])
+    in_copies[1].wait()
+    local_grad = by_group(gout)
+    a_buf[1] = local_grad.reshape(8, 16, D)
+    w3_copy.wait()
+    a_buf[2] = nt(local_grad, w3[...]).astype(BF16).reshape(8, 16, D)
+    spread(2, bg)
+    spread(1, fg.at[1, m])
 
     def first(t):
-        for d in range(1, 8):
-            slot = fg.at[t, m, behind(g, d)]
-            remote(slot, slot, sa_s.at[t, d], sa_r.at[t, d], over_g(behind(g, d))).wait_recv()
+        gathered(t, fg.at[t, m])
         for ss, rs, mm in ((sx_s, sx_r, side_m), (sc_s, sc_r, core_m)):
             copy = remote(fg.at[t, m], fg.at[t, m], ss.at[t], rs.at[t], mate(mm))
             copy.start()
@@ -159,11 +171,38 @@
         copy.start()
         sends.append(copy)
 
-    def third(t):
+    def from_core(t):
         slot = fg.at[t, core_m]
         remote(slot, slot, sc_s.at[t], sc_r.at[t], mate(core_m)).wait_recv()
+
+    def from_far(t):
         slot = fg.at[t, far_m]
         remote(slot, slot, sf_s.at[t], sf_r.at[t], mate(core_m)).wait_recv()
+
+    def project(mm):
+        f32 = fg[0, mm].reshape(128, D).astype(F32)
+        inverse = lax.rsqrt(jnp.mean(f32 * f32, -1, keepdims=True) + EPS)
+        normed_b = (f32 * inverse).astype(BF16)
+        na[mm] = normed_b
+        for j in range(3):
+            qa[j, mm] = nn(normed_b, ww[j]).astype(BF16)
+
+    first(0)
+    for copy in in_copies[2:] + win_copies:
+        copy.wait()
+    project(m)
+    from_core(0)
+    project(core_m)
+
+    def window(mm):
+        return bg.at[:, :, pl.ds(pl.multiple_of(128 * lax.div(3 * mm, 2), 128), WIN)]
+
+    gathered(2, bg)
+    for d, mm in ((1, side_m), (2, far_m), (3, core_m)):
+        copy = remote(window(mm), bx.at[m], sh_s.at[d], sh_r.at[d], mate(mm))
+        copy.start()
+        sends.append(copy)
+    second(0)
 
     nat = iota((READS, READS), 0)
     gs_v, ms_v, r_v = (nat >> 2) & 7, nat >> 5, nat & 3
@@ -177,29 +216,25 @@
         col = (32 * pi + 4 * g + k).astype(F32)
         return jnp.where(col >= begin, 1.0, 0.0) * jnp.where(col < close, 1.0, 0.0)
 
-    def to_columns(k):
-        return hot(iota((READS, 512), 1) == iota((READS, 512), 0) * 4 + k)
-
-    first(0)
-    second(0)
-    first(1)
-    third(0)
-    for copy in win_copies:
-        copy.wait()
-
-    for k in range(4):
-        f32 = nn(to_columns(k), fg[0].reshape(512, D))
-        fp[k] = f32.astype(BF16)
-        inverse = lax.rsqrt(jnp.mean(f32 * f32, -1, keepdims=True) + EPS)
-        normed_b = (f32 * inverse).astype(BF16)
-        nb[k] = normed_b
-        keep = cover(k)
+    project(side_m)
+    bx[m] = bg[:, :, pl.ds(off, WIN)]
+    pr, pc = iota((256, 512), 0), iota((256, 512), 1)
+
+    def to_columns(half):
+        return hot(pc == (pr & 127) * 4 + (pr >> 7) + 2 * half)
+
+    def set_heads(j, half, part):
+        for k in range(2):
+            for t in range(2):
+                at = (2 * half + k) * 128
+                heads[j, t, :, at : at + 128] = part[k * 128 : (k + 1) * 128, t * 128 : (t + 1) * 128]
+
+    from_far(0)
+    project(far_m)
+    for half in range(2):
+        keep = jnp.concatenate([cover(2 * half), cover(2 * half + 1)], axis=0)
         for j in range(3):
-            part = (nn(normed_b, ww[j]) * keep).astype(BF16)
-            heads[j, 0, :, k * 128 : (k + 1) * 128] = part[:, :128]
-            heads[j, 1, :, k * 128 : (k + 1) * 128] = part[:, 128:]
-        if k == 2:
-            second(1)
+            set_heads(j, half, (nn(to_columns(half), qa[j].reshape(512, WIN)) * keep).astype(BF16))
 
     low = jnp.where((iota((1, 512), 1) & 127) < 64, 1.0, 0.0)
     high = 1.0 - low
@@ -220,13 +255,16 @@
             sends.append(copy)
 
     scores(0, 0, 1)
-    third(1)
-    back = nt(fg[1].reshape(512, D), w3[...]).astype(BF16)
-    for k in range(4):
-        part = nn(to_columns(k), back).astype(BF16)
-        heads[3, 0, :, k * 128 : (k + 1) * 128] = part[:, :128]
-        heads[3, 1, :, k * 128 : (k + 1) * 128] = part[:, 128:]
+    for d, mm in ((1, side_m), (2, far_m), (3, core_m)):
+        remote(window(mm), bx.at[mm], sh_s.at[d], sh_r.at[d], mate(mm)).wait_recv()
+    for half in range(2):
+        set_heads(3, half, nn(to_columns(half), bx[...].reshape(512, WIN)).astype(BF16))
     scores(1, 3, 2)
+
+    first(1)
+    for half in range(2):
+        nb[2 * half : 2 * half + 2] = nn(to_columns(half), na[...].reshape(512, D)).astype(BF16).reshape(2, READS, D)
+    mine[...] = nn(hot(co == (ro & 31) * 4 + (ro >> 5)), fg[0, m].reshape(128, D)).astype(BF16)
 
     def turn(i, carry):
         w, col = iota((96, D), 0), iota((96, D), 1)
@@ -240,8 +278,6 @@
         return carry
 
     lax.fori_loop(0, 8, turn, 0)
-    for k in range(4):
-        gp[k] = nn(to_columns(k), fg[1].reshape(512, D)).astype(BF16)
 
     for which in range(2):
         total = lbuf[which, pl.ds(pl.multiple_of(48 * e, 16), 48), :]
@@ -263,6 +299,7 @@
 
         late.append((place, copy))
 
+    second(1)
     for o, place in enumerate(OWNERS):
         rows = pl.ds(pl.multiple_of(48 * e + 16 * o, 16), 16)
 
@@ -303,6 +340,10 @@
         copy.start()
         sends.append(copy)
     keeps = jnp.concatenate([jnp.broadcast_to(cover(k), (READS, 128)) for k in range(4)], axis=1)
+    from_core(1)
+    from_far(1)
+    for half in range(2):
+        gp[2 * half : 2 * half + 2] = nn(to_columns(half), fg[1].reshape(512, D)).astype(BF16).reshape(2, READS, D)
     for d in range(1, 8):
         ee = behind(e, d)
         remote(chunk(ee), chunk(ee), sp_s.at[d], sp_r.at[d], over_e(ee)).wait_recv()
@@ -385,9 +426,9 @@
         lane = 128 * ((3 * mm) // 2)
         for j in range(3):
             grad_norm = grad_norm + nt(rg[mm, j].reshape(128, WIN), wv[j, :, lane : lane + WIN])
-    mine = fp[:, rows_of(m), :].reshape(128, D).astype(F32)
-    inverse = lax.rsqrt(jnp.mean(mine * mine, -1, keepdims=True) + EPS)
-    normed = mine * inverse
+    own_feat = mine[...].astype(F32)
+    inverse = lax.rsqrt(jnp.mean(own_feat * own_feat, -1, keepdims=True) + EPS)
+    normed = own_feat * inverse
     result = (inverse * (grad_norm - normed * jnp.mean(grad_norm * normed, -1, keepdims=True))).astype(BF16)
     to_sources = hot(co == (ro & 3) * 32 + (ro >> 2))
     gi[...] = nn(to_sources, result).astype(BF16).reshape(8, 16, D)
@@ -429,8 +470,6 @@
         remote(slot, slot, si_s.at[d], si_r.at[d], over_g(behind(g, d))).wait_recv()
     from_groups = hot(co == ((ro >> 2) & 7) * 16 + (ro >> 5) * 4 + (ro & 3))
     gin[...] = nn(from_groups, ogi[...].reshape(128, D)).astype(BF16).reshape(4, 32, D)
-    gin_copy = pltpu.make_async_copy(gin, gin_out, s_in.at[0])
-    gin_copy.start()
 
     total = yb[0].astype(F32)
     for d in range(1, 8):
@@ -481,13 +520,9 @@
         for tile in range(6):
             wsum[:, j * D + tile * 128 : j * D + (tile + 1) * 128] = tiles[tile]
     wsum[:, 3 * D : 4 * D] = r3[0:3, :]
-    wsum_copy = pltpu.make_async_copy(wsum, wgrad_out, s_in.at[1])
-    wsum_copy.start()
 
     for copy in sends:
         copy.wait_send()
-    gin_copy.wait()
-    wsum_copy.wait()
     for place, copy in late:
 
         @pl.when(ze != place)
@@ -495,31 +530,42 @@
             copy.wait_send()
 
 
+def hand_over(gin, wgrad, gin_out, wgrad_out, sem):
+    copies = [pltpu.make_async_copy(gin, gin_out, sem.at[0]), pltpu.make_async_copy(wgrad, wgrad_out, sem.at[1])]
+    for copy in copies:
+        copy.start()
+    for copy in copies:
+        copy.wait()
+
+
 def shards(features, grad_out, weights, read_start, read_end):
     hbm = pl.BlockSpec(memory_space=pl.ANY)
+    vm = pl.BlockSpec(memory_space=pltpu.VMEM)
     dma = pltpu.SemaphoreType.DMA
-    return pl.pallas_call(
+    results = pl.pallas_call(
         kernel,
         name="tied_rows",
         out_shape=(
-            jax.ShapeDtypeStruct((4, 32, D), BF16),
-            jax.ShapeDtypeStruct((3, 4 * D), F32),
+            pltpu.VMEM((4, 32, D), BF16),
+            pltpu.VMEM((3, 4 * D), F32),
         ),
         in_specs=[hbm] * 5,
-        out_specs=(hbm, hbm),
+        out_specs=(vm, vm),
         scratch_shapes=[
             pltpu.VMEM((4, 32, D), BF16),
             pltpu.VMEM((4, 32, D), BF16),
             pltpu.VMEM((1, READS), I32),
             pltpu.VMEM((1, READS), I32),
-            pltpu.VMEM((4, 32, D), BF16),
-            pltpu.VMEM((3, 4 * D), F32),
             pltpu.VMEM((3, D, D), BF16),
             pltpu.VMEM((3, D, WIN), BF16),
-            pltpu.VMEM((WIN, D), BF16),
-            pltpu.VMEM((2, 8, 16, D), BF16),
+            pltpu.VMEM((D, D), BF16),
+            pltpu.VMEM((3, 8, 16, D), BF16),
             pltpu.VMEM((2, 4, 8, 16, D), BF16),
+            pltpu.VMEM((8, 16, D), BF16),
+            pltpu.VMEM((4, 8, 16, WIN), BF16),
+            pltpu.VMEM((3, 4, READS, WIN), BF16),
             pltpu.VMEM((4, READS, D), BF16),
+            pltpu.VMEM((READS, D), BF16),
             pltpu.VMEM((4, READS, D), BF16),
             pltpu.VMEM((4, READS, D), BF16),
             pltpu.VMEM((4, 2, READS, 512), BF16),
@@ -549,7 +595,7 @@
             pltpu.VMEM((8, 16, D), BF16),
             pltpu.VMEM((8, 16, D), BF16),
             dma((4,)), dma((7,)),
-            dma((2, 8)), dma((2, 8)), dma((2,)), dma((2,)), dma((2,)), dma((2,)), dma((2,)), dma((2,)),
+            dma((3, 8)), dma((3, 8)), dma((4,)), dma((4,)), dma((2,)), dma((2,)), dma((2,)), dma((2,)), dma((2,)), dma((2,)),
             dma((2, 8)), dma((2, 8)),
             dma((3,)), dma((8,)),
             dma((8,)), dma((3,)),
@@ -567,6 +613,15 @@
             collective_id=0, has_side_effects=True, vmem_limit_bytes=56 * 1024 * 1024
         ),
     )(features, grad_out, read_start.reshape(1, READS), read_end.reshape(1, READS), weights)
+    return pl.pallas_call(
+        hand_over,
+        name="hand_over",
+        out_shape=tuple(jax.ShapeDtypeStruct(r.shape, r.dtype) for r in results),
+        in_specs=[vm, vm],
+        out_specs=(hbm, hbm),
+        scratch_shapes=[dma((2,))],
+        compiler_params=pltpu.CompilerParams(vmem_limit_bytes=4 * 1024 * 1024),
+    )(*results)
 
 
 def solution(mesh):

time: 83.8 us -> 76.9 us (0.918)
  Pallas kernels: 80 us -> 76.2 us
  local copies, waits for them, and re-layouts: 3.04 us -> 0 us
    pallas_call x1 -> x2, Pallas kernels: 80 us -> 76.2 us  [the longest x1 75.5 us: shards(): pl.pallas_call(kernel, name='tied_rows', out_shape=(pltpu.VMEM((4, 32, D)...]
    unnamed x2 -> x0, local copies, waits for them, and re-layouts: 3.04 us -> none
where the time goes in v4:
time: 76.9 us; the launch traced here: 76.8 us
  Pallas kernels  76.2 us (99%)
    pallas_call x1, Pallas kernels, shards(): pl.pallas_call(kernel, name='tied_rows', out_shape=(pltpu.VMEM((4, 32, D)...  75.5 us

profile of v4, /device:TPU:1, one launch (start us, length us, event | category | flops | bytes accessed | tf_op | source)
XLA Modules:
  0.0 76.8 jit_solution(14085607160128574223)
XLA Ops:
  0.6 75.5 %tied_rows.1 = (bf16[4,32,768]{2,1,0:T(8,128)(2,1)S(1)}, f32[3,3072]{1,0:T(4,128)S(1)}) custom-call(bf16[4,32,768]{2,1,0:T(8,128)(2,1)} %feat_hbm.1, bf16[4,32,768]{2,1,0:T(8,128)(2,1)} %gout_hbm.1, s32[1,128]{1,0:T(1,128)} %bitcast.2, s32[1,128]{1,0:T(1,128)} %bitcast.3, bf16[4,768,768]{2,1,0:T(8,128)(2,1)} %w_hbm.1), custom_call_target="tpu_custom_call" | custom-call | tf_op jit(solution)/shard_map/tied_rows/pallas_call | solution.py:545
  76.1 0.7 hand_over.1

commit v5 on v4

--- a/solution.py
+++ b/solution.py
@@ -10,6 +10,7 @@
 F32, BF16, I32 = jnp.float32, jnp.bfloat16, jnp.int32
 D = 768
 WIN = 256
+PARTS = ((0, 384), (384, 256))
 PACK = 640
 READS = 128
 SCALE = 1.0 / 128.0
@@ -42,7 +43,7 @@
 def kernel(
     feat_hbm, gout_hbm, starts_hbm, ends_hbm, w_hbm, gin, wsum,
     feat, gout, starts, ends, wv, ww, w3, a_buf, fg, bg, bx, qa, na, mine, gp, nb, heads, lbuf, rl, acc, rz, pm,
-    gr, gpk, ob, rg, nbt, obt, wa, ra, wb, rb, za, rza, yb, ryb, fd, rj, f3, r3, gi, ogi,
+    gr, gpk, ob, rg, nbt, obt, wa0, wa1, ra0, ra1, wb, rb, za0, za1, rza0, rza1, yb, ryb, fd, rj, f3, r3, gi, ogi,
     s_in, s_w, sa_s, sa_r, sh_s, sh_r, sc_s, sc_r, sx_s, sx_r, sf_s, sf_r, sl_s, sl_r, sz_s, sz_r,
     sq_s, sq_r, sp_s, sp_r, sg_s, sg_r, sd_s, sd_r, se_s, se_r, sb_s, sb_r, sy_s, sy_r, sj_s, sj_r, s3_s, s3_r, si_s, si_r,
 ):
@@ -83,8 +84,23 @@
     def behind(v, d):
         return lax.rem(v + 8 - d, 8)
 
+    z1, z0 = lax.div(zl, 2), lax.rem(zl, 2)
+
+    def twin(d):
+        a, b, q = z1, z0, xp
+        a = 1 - a if d & 4 else a
+        b = 1 - b if d & 2 else b
+        q = 1 - q if d & 1 else q
+        return a * 4 + b * 2 + q
+
+    NEAR, FAR = (1, 2, 3), (4, 5, 6, 7)
+
+    def side_of(ref, far):
+        return ref.at[pl.ds((1 - z1 if far else z1) * 4, 4)]
+
     turned = (read_of(m * 2 + xp, zl), pi)
     sends = []
+    wa, ra, za, rza = (wa0, wa1), (ra0, ra1), (za0, za1), (rza0, rza1)
 
     in_copies = [
         pltpu.make_async_copy(src, dst, s_in.at[i])
@@ -101,7 +117,7 @@
         pl.semaphore_signal(barrier, inc=1, device_id=dev, device_id_type=pl.DeviceIdType.MESH)
 
     for d in range(1, 8):
-        greet(over_g(ahead(g, d)))
+        greet(over_g(twin(d)))
         greet(over_e(ahead(e, d)))
         greet(over_z(ahead(ze, d)))
     for mm in (core_m, side_m, far_m):
@@ -125,17 +141,17 @@
         return nn(to_groups, ref[...].reshape(128, D)).astype(BF16)
 
     def spread(i, dst):
-        for d in range(1, 8):
-            gg = ahead(g, d)
+        dst[g] = a_buf[i, g]
+        for d in FAR + NEAR:
+            gg = twin(d)
             copy = remote(a_buf.at[i, gg], dst.at[g], sa_s.at[i, d], sa_r.at[i, d], over_g(gg))
             copy.start()
             sends.append(copy)
-        dst[g] = a_buf[i, g]
-
-    def gathered(i, dst):
-        for d in range(1, 8):
-            slot = dst.at[behind(g, d)]
-            remote(slot, slot, sa_s.at[i, d], sa_r.at[i, d], over_g(behind(g, d))).wait_recv()
+
+    def gathered(i, dst, far):
+        for d in FAR if far else NEAR:
+            slot = dst.at[twin(d)]
+            remote(slot, slot, sa_s.at[i, d], sa_r.at[i, d], over_g(twin(d))).wait_recv()
 
     in_copies[0].wait()
     a_buf[0] = by_group(feat).reshape(8, 16, D)
@@ -157,27 +173,30 @@
     spread(2, bg)
     spread(1, fg.at[1, m])
 
-    def first(t):
-        gathered(t, fg.at[t, m])
+    def first(t, far):
+        gathered(t, fg.at[t, m], far)
+        slot = side_of(fg.at[t, m], far)
         for ss, rs, mm in ((sx_s, sx_r, side_m), (sc_s, sc_r, core_m)):
-            copy = remote(fg.at[t, m], fg.at[t, m], ss.at[t], rs.at[t], mate(mm))
+            copy = remote(slot, slot, ss.at[t, far], rs.at[t, far], mate(mm))
             copy.start()
             sends.append(copy)
 
-    def second(t):
-        slot = fg.at[t, side_m]
-        remote(slot, slot, sx_s.at[t], sx_r.at[t], mate(side_m)).wait_recv()
-        copy = remote(slot, slot, sf_s.at[t], sf_r.at[t], mate(core_m))
+    def second(t, far):
+        slot = side_of(fg.at[t, side_m], far)
+        remote(slot, slot, sx_s.at[t, far], sx_r.at[t, far], mate(side_m)).wait_recv()
+        copy = remote(slot, slot, sf_s.at[t, far], sf_r.at[t, far], mate(core_m))
         copy.start()
         sends.append(copy)
 
     def from_core(t):
-        slot = fg.at[t, core_m]
-        remote(slot, slot, sc_s.at[t], sc_r.at[t], mate(core_m)).wait_recv()
+        for far in (0, 1):
+            slot = side_of(fg.at[t, core_m], far)
+            remote(slot, slot, sc_s.at[t, far], sc_r.at[t, far], mate(core_m)).wait_recv()
 
     def from_far(t):
-        slot = fg.at[t, far_m]
-        remote(slot, slot, sf_s.at[t], sf_r.at[t], mate(core_m)).wait_recv()
+        for far in (0, 1):
+            slot = side_of(fg.at[t, far_m], far)
+            remote(slot, slot, sf_s.at[t, far], sf_r.at[t, far], mate(core_m)).wait_recv()
 
     def project(mm):
         f32 = fg[0, mm].reshape(128, D).astype(F32)
@@ -187,23 +206,29 @@
         for j in range(3):
             qa[j, mm] = nn(normed_b, ww[j]).astype(BF16)
 
-    first(0)
+    first(0, 0)
     for copy in in_copies[2:] + win_copies:
         copy.wait()
+    first(0, 1)
+    second(0, 0)
     project(m)
     from_core(0)
     project(core_m)
 
-    def window(mm):
-        return bg.at[:, :, pl.ds(pl.multiple_of(128 * lax.div(3 * mm, 2), 128), WIN)]
-
-    gathered(2, bg)
-    for d, mm in ((1, side_m), (2, far_m), (3, core_m)):
-        copy = remote(window(mm), bx.at[m], sh_s.at[d], sh_r.at[d], mate(mm))
-        copy.start()
-        sends.append(copy)
-    second(0)
-
+    def window(mm, far):
+        lane = pl.multiple_of(128 * lax.div(3 * mm, 2), 128)
+        return side_of(bg, far).at[:, :, pl.ds(lane, WIN)]
+
+    def trade(far):
+        gathered(2, bg, far)
+        for d, mm in ((1, side_m), (2, far_m), (3, core_m)):
+            copy = remote(window(mm, far), side_of(bx.at[m], far), sh_s.at[far, d], sh_r.at[far, d], mate(mm))
+            copy.start()
+            sends.append(copy)
+
+    trade(0)
+    second(0, 1)
+    trade(1)
     nat = iota((READS, READS), 0)
     gs_v, ms_v, r_v = (nat >> 2) & 7, nat >> 5, nat & 3
     xi_v, xp_v = ms_v >> 1, gs_v & 1
@@ -255,29 +280,34 @@
             sends.append(copy)
 
     scores(0, 0, 1)
-    for d, mm in ((1, side_m), (2, far_m), (3, core_m)):
-        remote(window(mm), bx.at[mm], sh_s.at[d], sh_r.at[d], mate(mm)).wait_recv()
+    for far in (0, 1):
+        for d, mm in ((1, side_m), (2, far_m), (3, core_m)):
+            slot = side_of(bx.at[mm], far)
+            remote(slot, slot, sh_s.at[far, d], sh_r.at[far, d], mate(mm)).wait_recv()
     for half in range(2):
         set_heads(3, half, nn(to_columns(half), bx[...].reshape(512, WIN)).astype(BF16))
     scores(1, 3, 2)
 
-    first(1)
+    first(1, 0)
+    first(1, 1)
     for half in range(2):
         nb[2 * half : 2 * half + 2] = nn(to_columns(half), na[...].reshape(512, D)).astype(BF16).reshape(2, READS, D)
     mine[...] = nn(hot(co == (ro & 31) * 4 + (ro >> 5)), fg[0, m].reshape(128, D)).astype(BF16)
 
-    def turn(i, carry):
+    def turn(half):
         w, col = iota((96, D), 0), iota((96, D), 1)
-        yy, xx = lax.div(ahead(e, i + 1), 2), lax.rem(ahead(e, i + 1), 2)
         xi2 = (w >> 1) & 1
-        row = (
-            ((w >> 3) & 3) * 192 + (xi2 + xx * (3 - 2 * xi2)) * 48 + (w & 1) * 24
-            + yy * 6 + ((w >> 2) & 1) * 3 + (w >> 5)
-        )
-        nbt[pl.ds(pl.multiple_of(i * 96, 16), 96), :] = nt(hot(col == row), nb[...].reshape(512, D)).astype(BF16)
-        return carry
-
-    lax.fori_loop(0, 8, turn, 0)
+        picks = []
+        for q in range(4):
+            ee = ahead(e, half * 4 + q + 1)
+            yy, xx = lax.div(ee, 2), lax.rem(ee, 2)
+            row = (
+                ((w >> 3) & 3) * 192 + (xi2 + xx * (3 - 2 * xi2)) * 48 + (w & 1) * 24
+                + yy * 6 + ((w >> 2) & 1) * 3 + (w >> 5)
+            )
+            picks.append(hot(col == row))
+        pick = jnp.concatenate(picks, axis=0)
+        nbt[half * 384 : (half + 1) * 384, :] = nt(pick, nb[...].reshape(512, D)).astype(BF16)
 
     for which in range(2):
         total = lbuf[which, pl.ds(pl.multiple_of(48 * e, 16), 48), :]
@@ -299,7 +329,9 @@
 
         late.append((place, copy))
 
-    second(1)
+    second(1, 0)
+    second(1, 1)
+    turn(0)
     for o, place in enumerate(OWNERS):
         rows = pl.ds(pl.multiple_of(48 * e + 16 * o, 16), 16)
 
@@ -325,6 +357,7 @@
             for copy in out:
                 copy.wait_send()
 
+    turn(1)
     for o, place in enumerate(OWNERS):
         rows = pl.ds(pl.multiple_of(48 * e + 16 * o, 16), 16)
 
@@ -393,19 +426,21 @@
         sends.append(copy)
     rg[m] = gr[:, :, rows_of(m), :]
 
-    right = gpk[...].reshape(512, PACK)
-    for half in range(2):
-        part = nn(nbt[half * 384 : (half + 1) * 384, :], right).astype(BF16)
-        for q in range(4):
-            d = (half * 4 + q + 1) % 8
-            wa[d] = part[q * 96 : (q + 1) * 96, :]
-        for q in range(4):
-            d = (half * 4 + q + 1) % 8
-            if d > 0:
-                copy = remote(wa.at[d], ra.at[d], sd_s.at[d], sd_r.at[d], over_e(ahead(e, d)))
-                copy.start()
-                sends.append(copy)
-
+    def left_parts(p):
+        first_lane, count = PARTS[p]
+        right = gpk[:, :, first_lane : first_lane + count].reshape(512, count)
+        for half in range(2):
+            part = nn(nbt[half * 384 : (half + 1) * 384, :], right).astype(BF16)
+            for q in range(4):
+                wa[p][(half * 4 + q + 1) % 8] = part[q * 96 : (q + 1) * 96, :]
+            for q in range(4):
+                d = (half * 4 + q + 1) % 8
+                if d > 0:
+                    copy = remote(wa[p].at[d], ra[p].at[d], sd_s.at[p, d], sd_r.at[p, d], over_e(ahead(e, d)))
+                    copy.start()
+                    sends.append(copy)
+
+    left_parts(0)
     ow, cw = iota((256, 256), 0), iota((256, 256), 1)
     u, zz = ow & 31, ((ow >> 5) + ze) & 7
     xi2, xx, yy = (zz >> 1) & 1, u & 1, (u >> 1) & 3
@@ -416,6 +451,8 @@
         copy = remote(wb.at[d], rb.at[d], sb_s.at[d], sb_r.at[d], over_z(ahead(ze, d)))
         copy.start()
         sends.append(copy)
+
+    left_parts(1)
 
     for d, mm in ((1, side_m), (2, far_m), (3, core_m)):
         remote(gr.at[:, :, rows_of(mm), :], rg.at[mm], sg_s.at[d], sg_r.at[d], mate(mm)).wait_recv()
@@ -432,13 +469,29 @@
     result = (inverse * (grad_norm - normed * jnp.mean(grad_norm * normed, -1, keepdims=True))).astype(BF16)
     to_sources = hot(co == (ro & 3) * 32 + (ro >> 2))
     gi[...] = nn(to_sources, result).astype(BF16).reshape(8, 16, D)
-    for d in range(1, 8):
-        gg = ahead(g, d)
+    for d in FAR + NEAR:
+        gg = twin(d)
         copy = remote(gi.at[gg], ogi.at[g], si_s.at[d], si_r.at[d], over_g(gg))
         copy.start()
         sends.append(copy)
     ogi[g] = gi[g]
 
+    def second_parts(p):
+        count = PARTS[p][1]
+        total = wa[p][0].astype(F32)
+        for d in range(1, 8):
+            remote(ra[p].at[d], ra[p].at[d], sd_s.at[p, d], sd_r.at[p, d], over_e(behind(e, d))).wait_recv()
+            total = total + ra[p][d].astype(F32)
+        ra_row, ra_col = iota((128, 96), 0), iota((128, 96), 1)
+        v, zz = ra_row & 15, ((ra_row >> 4) + ze) & 7
+        src = jnp.where(v < 12, (v >> 2) * 32 + (zz & 3) * 8 + (zz >> 2) * 4 + (v & 3), -1)
+        za[p][...] = nn(hot(ra_col == src), total.astype(BF16)).astype(BF16).reshape(8, 16, count)
+        for d in range(1, 8):
+            copy = remote(za[p].at[d], rza[p].at[d], se_s.at[p, d], se_r.at[p, d], over_z(ahead(ze, d)))
+            copy.start()
+            sends.append(copy)
+
+    second_parts(0)
     total = wb[0].astype(F32)
     for d in range(1, 8):
         remote(rb.at[d], rb.at[d], sb_s.at[d], sb_r.at[d], over_z(behind(ze, d))).wait_recv()
@@ -452,22 +505,11 @@
         copy.start()
         sends.append(copy)
 
-    total = wa[0].astype(F32)
-    for d in range(1, 8):
-        remote(ra.at[d], ra.at[d], sd_s.at[d], sd_r.at[d], over_e(behind(e, d))).wait_recv()
-        total = total + ra[d].astype(F32)
-    ra_row, ra_col = iota((128, 96), 0), iota((128, 96), 1)
-    v, zz = ra_row & 15, ((ra_row >> 4) + ze) & 7
-    src = jnp.where(v < 12, (v >> 2) * 32 + (zz & 3) * 8 + (zz >> 2) * 4 + (v & 3), -1)
-    za[...] = nn(hot(ra_col == src), total.astype(BF16)).astype(BF16).reshape(8, 16, PACK)
-    for d in range(1, 8):
-        copy = remote(za.at[d], rza.at[d], se_s.at[d], se_r.at[d], over_z(ahead(ze, d)))
-        copy.start()
-        sends.append(copy)
-
-    for d in range(1, 8):
-        slot = ogi.at[behind(g, d)]
-        remote(slot, slot, si_s.at[d], si_r.at[d], over_g(behind(g, d))).wait_recv()
+    second_parts(1)
+
+    for d in range(1, 8):
+        slot = ogi.at[twin(d)]
+        remote(slot, slot, si_s.at[d], si_r.at[d], over_g(twin(d))).wait_recv()
     from_groups = hot(co == ((ro >> 2) & 7) * 16 + (ro >> 5) * 4 + (ro & 3))
     gin[...] = nn(from_groups, ogi[...].reshape(128, D)).astype(BF16).reshape(4, 32, D)
 
@@ -486,14 +528,15 @@
     def _():
         r3[...] = f3[...]
 
-    total = za[0].astype(F32)
-    for d in range(1, 8):
-        remote(rza.at[d], rza.at[d], se_s.at[d], se_r.at[d], over_z(behind(ze, d))).wait_recv()
-        total = total + rza[d].astype(F32)
-    for mm in range(4):
-        for t in range(3):
-            fd[mm, t : t + 1, :] = total[t * 4 + mm : t * 4 + mm + 1, :]
-        fd[mm, 3:8, :] = jnp.zeros((5, PACK), F32)
+    for p, (lane, count) in enumerate(PARTS):
+        total = za[p][0].astype(F32)
+        for d in range(1, 8):
+            remote(rza[p].at[d], rza[p].at[d], se_s.at[p, d], se_r.at[p, d], over_z(behind(ze, d))).wait_recv()
+            total = total + rza[p][d].astype(F32)
+        for mm in range(4):
+            for t in range(3):
+                fd[mm, t : t + 1, lane : lane + count] = total[t * 4 + mm : t * 4 + mm + 1, :]
+            fd[mm, 3:8, lane : lane + count] = jnp.zeros((5, count), F32)
     for d, mm in ((1, side_m), (2, far_m), (3, core_m)):
         copy = remote(fd.at[mm], rj.at[m], sj_s.at[d], sj_r.at[d], mate(mm))
         copy.start()
@@ -580,12 +623,16 @@
             pltpu.VMEM((4, 3, 4, 32, WIN), BF16),
             pltpu.VMEM((D, 512), BF16),
             pltpu.VMEM((WIN, 512), BF16),
-            pltpu.VMEM((8, 96, PACK), BF16),
-            pltpu.VMEM((8, 96, PACK), BF16),
+            pltpu.VMEM((8, 96, PARTS[0][1]), BF16),
+            pltpu.VMEM((8, 96, PARTS[1][1]), BF16),
+            pltpu.VMEM((8, 96, PARTS[0][1]), BF16),
+            pltpu.VMEM((8, 96, PARTS[1][1]), BF16),
             pltpu.VMEM((8, 32, D), BF16),
             pltpu.VMEM((8, 32, D), BF16),
-            pltpu.VMEM((8, 16, PACK), BF16),
-            pltpu.VMEM((8, 16, PACK), BF16),
+            pltpu.VMEM((8, 16, PARTS[0][1]), BF16),
+            pltpu.VMEM((8, 16, PARTS[1][1]), BF16),
+            pltpu.VMEM((8, 16, PARTS[0][1]), BF16),
+            pltpu.VMEM((8, 16, PARTS[1][1]), BF16),
             pltpu.VMEM((8, 16, D), BF16),
             pltpu.VMEM((8, 16, D), BF16),
             pltpu.VMEM((4, 8, PACK), F32),
@@ -595,14 +642,15 @@
             pltpu.VMEM((8, 16, D), BF16),
             pltpu.VMEM((8, 16, D), BF16),
             dma((4,)), dma((7,)),
-            dma((3, 8)), dma((3, 8)), dma((4,)), dma((4,)), dma((2,)), dma((2,)), dma((2,)), dma((2,)), dma((2,)), dma((2,)),
+            dma((3, 8)), dma((3, 8)), dma((2, 4)), dma((2, 4)),
+            dma((2, 2)), dma((2, 2)), dma((2, 2)), dma((2, 2)), dma((2, 2)), dma((2, 2)),
             dma((2, 8)), dma((2, 8)),
             dma((3,)), dma((8,)),
             dma((8,)), dma((3,)),
             dma((8,)), dma((8,)),
             dma((4,)), dma((4,)),
-            dma((8,)), dma((8,)),
-            dma((8,)), dma((8,)),
+            dma((2, 8)), dma((2, 8)),
+            dma((2, 8)), dma((2, 8)),
             dma((8,)), dma((8,)),
             dma((8,)), dma((8,)),
             dma((4,)), dma((4,)),

time: 76.9 us -> 75.8 us (0.986)
  Pallas kernels: 76.2 us -> 75 us
    pallas_call x1, Pallas kernels: 75.5 us -> 74.3 us  [shards(): pl.pallas_call(kernel, name='tied_rows', out_shape=(pltpu.VMEM((4, 32, D)...]
where the time goes in v5:
time: 75.8 us; the launch traced here: 75.7 us
  Pallas kernels  75 us (99%)
    pallas_call x1, Pallas kernels, shards(): pl.pallas_call(kernel, name='tied_rows', out_shape=(pltpu.VMEM((4, 32, D)...  74.3 us

profile of v5, /device:TPU:1, one launch (start us, length us, event | category | flops | bytes accessed | tf_op | source)
XLA Modules:
  0.0 75.7 jit_solution(10895597128044799896)
XLA Ops:
  0.6 74.3 %tied_rows.1 = (bf16[4,32,768]{2,1,0:T(8,128)(2,1)S(1)}, f32[3,3072]{1,0:T(4,128)S(1)}) custom-call(bf16[4,32,768]{2,1,0:T(8,128)(2,1)} %feat_hbm.1, bf16[4,32,768]{2,1,0:T(8,128)(2,1)} %gout_hbm.1, s32[1,128]{1,0:T(1,128)} %bitcast.2, s32[1,128]{1,0:T(1,128)} %bitcast.3, bf16[4,768,768]{2,1,0:T(8,128)(2,1)} %w_hbm.1), custom_call_target="tpu_custom_call" | custom-call | tf_op jit(solution)/shard_map/tied_rows/pallas_call | solution.py:588
  75.0 0.7 hand_over.1

commit v6 on v5

--- a/solution.py
+++ b/solution.py
@@ -42,7 +42,7 @@
 
 def kernel(
     feat_hbm, gout_hbm, starts_hbm, ends_hbm, w_hbm, gin, wsum,
-    feat, gout, starts, ends, wv, ww, w3, a_buf, fg, bg, bx, qa, na, mine, gp, nb, heads, lbuf, rl, acc, rz, pm,
+    feat, gout, starts, ends, wv, ww, w3, a_buf, fg, to_columns, bg, bx, qa, na, mine, gp, nb, heads, lbuf, rl, acc, rz, pm,
     gr, gpk, ob, rg, nbt, obt, wa0, wa1, ra0, ra1, wb, rb, za0, za1, rza0, rza1, yb, ryb, fd, rj, f3, r3, gi, ogi,
     s_in, s_w, sa_s, sa_r, sh_s, sh_r, sc_s, sc_r, sx_s, sx_r, sf_s, sf_r, sl_s, sl_r, sz_s, sz_r,
     sq_s, sq_r, sp_s, sp_r, sg_s, sg_r, sd_s, sd_r, se_s, se_r, sb_s, sb_r, sy_s, sy_r, sj_s, sj_r, s3_s, s3_r, si_s, si_r,
@@ -206,6 +206,9 @@
         for j in range(3):
             qa[j, mm] = nn(normed_b, ww[j]).astype(BF16)
 
+    for k in range(4):
+        pr, pc = iota((READS, 512), 0), iota((READS, 512), 1)
+        to_columns[k * 128 : (k + 1) * 128, :] = hot(pc == pr * 4 + k)
     first(0, 0)
     for copy in in_copies[2:] + win_copies:
         copy.wait()
@@ -243,23 +246,16 @@
 
     project(side_m)
     bx[m] = bg[:, :, pl.ds(off, WIN)]
-    pr, pc = iota((256, 512), 0), iota((256, 512), 1)
-
-    def to_columns(half):
-        return hot(pc == (pr & 127) * 4 + (pr >> 7) + 2 * half)
-
-    def set_heads(j, half, part):
-        for k in range(2):
+    def set_heads(j, part):
+        for k in range(4):
             for t in range(2):
-                at = (2 * half + k) * 128
-                heads[j, t, :, at : at + 128] = part[k * 128 : (k + 1) * 128, t * 128 : (t + 1) * 128]
-
+                heads[j, t, :, k * 128 : (k + 1) * 128] = part[k * 128 : (k + 1) * 128, t * 128 : (t + 1) * 128]
+
+    keep = jnp.concatenate([cover(k) for k in range(4)], axis=0)
     from_far(0)
     project(far_m)
-    for half in range(2):
-        keep = jnp.concatenate([cover(2 * half), cover(2 * half + 1)], axis=0)
-        for j in range(3):
-            set_heads(j, half, (nn(to_columns(half), qa[j].reshape(512, WIN)) * keep).astype(BF16))
+    for j in range(3):
+        set_heads(j, (nn(to_columns[...], qa[j].reshape(512, WIN)) * keep).astype(BF16))
 
     low = jnp.where((iota((1, 512), 1) & 127) < 64, 1.0, 0.0)
     high = 1.0 - low
@@ -284,14 +280,14 @@
         for d, mm in ((1, side_m), (2, far_m), (3, core_m)):
             slot = side_of(bx.at[mm], far)
             remote(slot, slot, sh_s.at[far, d], sh_r.at[far, d], mate(mm)).wait_recv()
-    for half in range(2):
-        set_heads(3, half, nn(to_columns(half), bx[...].reshape(512, WIN)).astype(BF16))
+    set_heads(3, nn(to_columns[...], bx[...].reshape(512, WIN)).astype(BF16))
     scores(1, 3, 2)
 
     first(1, 0)
     first(1, 1)
     for half in range(2):
-        nb[2 * half : 2 * half + 2] = nn(to_columns(half), na[...].reshape(512, D)).astype(BF16).reshape(2, READS, D)
+        rows = to_columns[half * 256 : (half + 1) * 256, :]
+        nb[2 * half : 2 * half + 2] = nn(rows, na[...].reshape(512, D)).astype(BF16).reshape(2, READS, D)
     mine[...] = nn(hot(co == (ro & 31) * 4 + (ro >> 5)), fg[0, m].reshape(128, D)).astype(BF16)
 
     def turn(half):
@@ -376,7 +372,8 @@
     from_core(1)
     from_far(1)
     for half in range(2):
-        gp[2 * half : 2 * half + 2] = nn(to_columns(half), fg[1].reshape(512, D)).astype(BF16).reshape(2, READS, D)
+        rows = to_columns[half * 256 : (half + 1) * 256, :]
+        gp[2 * half : 2 * half + 2] = nn(rows, fg[1].reshape(512, D)).astype(BF16).reshape(2, READS, D)
     for d in range(1, 8):
         ee = behind(e, d)
         remote(chunk(ee), chunk(ee), sp_s.at[d], sp_r.at[d], over_e(ee)).wait_recv()
@@ -441,6 +438,7 @@
                     sends.append(copy)
 
     left_parts(0)
+    left_parts(1)
     ow, cw = iota((256, 256), 0), iota((256, 256), 1)
     u, zz = ow & 31, ((ow >> 5) + ze) & 7
     xi2, xx, yy = (zz >> 1) & 1, u & 1, (u >> 1) & 3
@@ -451,30 +449,6 @@
         copy = remote(wb.at[d], rb.at[d], sb_s.at[d], sb_r.at[d], over_z(ahead(ze, d)))
         copy.start()
         sends.append(copy)
-
-    left_parts(1)
-
-    for d, mm in ((1, side_m), (2, far_m), (3, core_m)):
-        remote(gr.at[:, :, rows_of(mm), :], rg.at[mm], sg_s.at[d], sg_r.at[d], mate(mm)).wait_recv()
-    for copy in full_copies:
-        copy.wait()
-    grad_norm = jnp.zeros((128, D), F32)
-    for mm in range(4):
-        lane = 128 * ((3 * mm) // 2)
-        for j in range(3):
-            grad_norm = grad_norm + nt(rg[mm, j].reshape(128, WIN), wv[j, :, lane : lane + WIN])
-    own_feat = mine[...].astype(F32)
-    inverse = lax.rsqrt(jnp.mean(own_feat * own_feat, -1, keepdims=True) + EPS)
-    normed = own_feat * inverse
-    result = (inverse * (grad_norm - normed * jnp.mean(grad_norm * normed, -1, keepdims=True))).astype(BF16)
-    to_sources = hot(co == (ro & 3) * 32 + (ro >> 2))
-    gi[...] = nn(to_sources, result).astype(BF16).reshape(8, 16, D)
-    for d in FAR + NEAR:
-        gg = twin(d)
-        copy = remote(gi.at[gg], ogi.at[g], si_s.at[d], si_r.at[d], over_g(gg))
-        copy.start()
-        sends.append(copy)
-    ogi[g] = gi[g]
 
     def second_parts(p):
         count = PARTS[p][1]
@@ -490,6 +464,28 @@
             copy = remote(za[p].at[d], rza[p].at[d], se_s.at[p, d], se_r.at[p, d], over_z(ahead(ze, d)))
             copy.start()
             sends.append(copy)
+
+    for copy in full_copies:
+        copy.wait()
+    grad_norm = jnp.zeros((128, D), F32)
+    for d, mm in ((0, m), (3, core_m), (1, side_m), (2, far_m)):
+        if d > 0:
+            remote(gr.at[:, :, rows_of(mm), :], rg.at[mm], sg_s.at[d], sg_r.at[d], mate(mm)).wait_recv()
+        lane = pl.multiple_of(128 * lax.div(3 * mm, 2), 128)
+        for j in range(3):
+            grad_norm = grad_norm + nt(rg[mm, j].reshape(128, WIN), wv[j, :, pl.ds(lane, WIN)])
+    own_feat = mine[...].astype(F32)
+    inverse = lax.rsqrt(jnp.mean(own_feat * own_feat, -1, keepdims=True) + EPS)
+    normed = own_feat * inverse
+    result = (inverse * (grad_norm - normed * jnp.mean(grad_norm * normed, -1, keepdims=True))).astype(BF16)
+    to_sources = hot(co == (ro & 3) * 32 + (ro >> 2))
+    gi[...] = nn(to_sources, result).astype(BF16).reshape(8, 16, D)
+    for d in FAR + NEAR:
+        gg = twin(d)
+        copy = remote(gi.at[gg], ogi.at[g], si_s.at[d], si_r.at[d], over_g(gg))
+        copy.start()
+        sends.append(copy)
+    ogi[g] = gi[g]
 
     second_parts(0)
     total = wb[0].astype(F32)
@@ -604,6 +600,7 @@
             pltpu.VMEM((D, D), BF16),
             pltpu.VMEM((3, 8, 16, D), BF16),
             pltpu.VMEM((2, 4, 8, 16, D), BF16),
+            pltpu.VMEM((512, 512), BF16),
             pltpu.VMEM((8, 16, D), BF16),
             pltpu.VMEM((4, 8, 16, WIN), BF16),
             pltpu.VMEM((3, 4, READS, WIN), BF16),

time: 75.8 us -> 75.2 us (level)
  no operation moved by 1% of the time
where the time goes in v6:
time: 75.2 us; the launch traced here: 75.1 us
  Pallas kernels  74.5 us (99%)
    pallas_call x1, Pallas kernels, shards(): pl.pallas_call(kernel, name='tied_rows', out_shape=(pltpu.VMEM((4, 32, D)...  73.8 us

profile of v6, /device:TPU:1, one launch (start us, length us, event | category | flops | bytes accessed | tf_op | source)
XLA Modules:
  0.0 75.1 jit_solution(14391112172930030538)
XLA Ops:
  0.6 73.8 %tied_rows.1 = (bf16[4,32,768]{2,1,0:T(8,128)(2,1)S(1)}, f32[3,3072]{1,0:T(4,128)S(1)}) custom-call(bf16[4,32,768]{2,1,0:T(8,128)(2,1)} %feat_hbm.1, bf16[4,32,768]{2,1,0:T(8,128)(2,1)} %gout_hbm.1, s32[1,128]{1,0:T(1,128)} %bitcast.2, s32[1,128]{1,0:T(1,128)} %bitcast.3, bf16[4,768,768]{2,1,0:T(8,128)(2,1)} %w_hbm.1), custom_call_target="tpu_custom_call" | custom-call | tf_op jit(solution)/shard_map/tied_rows/pallas_call | solution.py:584
  74.4 0.7 hand_over.1

commit v7 on v6

--- a/solution.py
+++ b/solution.py
@@ -171,7 +171,6 @@
     w3_copy.wait()
     a_buf[2] = nt(local_grad, w3[...]).astype(BF16).reshape(8, 16, D)
     spread(2, bg)
-    spread(1, fg.at[1, m])
 
     def first(t, far):
         gathered(t, fg.at[t, m], far)
@@ -232,6 +231,7 @@
     trade(0)
     second(0, 1)
     trade(1)
+    spread(1, fg.at[1, m])
     nat = iota((READS, READS), 0)
     gs_v, ms_v, r_v = (nat >> 2) & 7, nat >> 5, nat & 3
     xi_v, xp_v = ms_v >> 1, gs_v & 1
@@ -284,11 +284,12 @@
     scores(1, 3, 2)
 
     first(1, 0)
-    first(1, 1)
     for half in range(2):
         rows = to_columns[half * 256 : (half + 1) * 256, :]
         nb[2 * half : 2 * half + 2] = nn(rows, na[...].reshape(512, D)).astype(BF16).reshape(2, READS, D)
     mine[...] = nn(hot(co == (ro & 31) * 4 + (ro >> 5)), fg[0, m].reshape(128, D)).astype(BF16)
+
+    first(1, 1)
 
     def turn(half):
         w, col = iota((96, D), 0), iota((96, D), 1)

time: 75.2 us -> 74.5 us (level)
  no operation moved by 1% of the time
where the time goes in v7:
time: 74.5 us; the launch traced here: 74.4 us
  Pallas kernels  73.8 us (99%)
    pallas_call x1, Pallas kernels, shards(): pl.pallas_call(kernel, name='tied_rows', out_shape=(pltpu.VMEM((4, 32, D)...  73.1 us

profile of v7, /device:TPU:1, one launch (start us, length us, event | category | flops | bytes accessed | tf_op | source)
XLA Modules:
  0.0 74.4 jit_solution(2040332197134013362)
XLA Ops:
  0.6 73.1 %tied_rows.1 = (bf16[4,32,768]{2,1,0:T(8,128)(2,1)S(1)}, f32[3,3072]{1,0:T(4,128)S(1)}) custom-call(bf16[4,32,768]{2,1,0:T(8,128)(2,1)} %feat_hbm.1, bf16[4,32,768]{2,1,0:T(8,128)(2,1)} %gout_hbm.1, s32[1,128]{1,0:T(1,128)} %bitcast.2, s32[1,128]{1,0:T(1,128)} %bitcast.3, bf16[4,768,768]{2,1,0:T(8,128)(2,1)} %w_hbm.1), custom_call_target="tpu_custom_call" | custom-call | tf_op jit(solution)/shard_map/tied_rows/pallas_call | solution.py:585
  73.7 0.7 hand_over.1
